TPU v7x, 512 devices: a whole 4x8x8 slice. The times are simulated.
512 devices in a mesh: seq: 64 (over y, z), head: 8 (over x, core).
Axes of the slice: x: 4, y: 8, z: 8, core: 2. Of those that a mesh axis runs over, the one named last changes fastest.
Arguments:
- queries: bfloat16 [16384, 4096], P(('seq', 'head'))
- key_values: bfloat16 [16384, 2, 1024], P(('seq', 'head'))
- gate_logits: bfloat16 [16384, 4096], P(('seq', 'head')), may hold values from -6 to 6
- vertical_blocks: int32 [32, 16], replicated, may hold values from 0 to 255, as said below
- slash_offsets: int32 [32, 8], replicated, may hold values from 0 to 8, as said below
- slash_count: int32 [32], replicated, may hold values from 2 to 8, as said below
Outputs:
- gated: bfloat16 [16384, 4096], P(('seq', 'head'))
Inputs may be any that keep to these rules, and one draw needn't show every extreme that they name: `slash_count`: between 2 and 8; the largest and the smallest are reached. Heads are ranked by (slash_count[h], h) ascending, and rank r goes to head group (r % 8) if (r // 8) is even, else to group 8 - 1 - (r % 8). For each head, slash_offsets[h, 0] = 0 and the 8 offsets are distinct; the largest possible offset is used by some head. `vertical_blocks`: each head's 16 blocks lie in distinct token shards of 256 tokens (block b is in shard b // 4); the heads of one group, as defined with slash_count, have at most 1 vertical blocks in one shard together, and exactly 1 in some shard. The first and the last block of the stretch are used by some head.
All inputs are finite; a program needn't handle non-finite values.
Results may differ from a plain program's by a relative error of at most 0.0057.
Values may be sent and summed in bfloat16 or wider, within the bound.
No kernel may reach another device: no remote copies, remote signals or barrier semaphores. Data moves between devices by JAX's collectives and lax.ppermute only.
A program may use at most 64 MiB of HBM per device.

v0:
```python
import jax
import jax.numpy as jnp
from jax import lax
from jax.sharding import PartitionSpec as P

H = 32
KVH = 8
DH = 128
BLOCK = 64
NS = 8
REACH = 2


def from_behind(value, axis, steps):
    count = lax.axis_size(axis)
    first, last = (max(0, -steps), min(count, count - steps))
    return lax.ppermute(value, axis, [(source, source + steps) for source in range(first, last)])


def block_attend(
    q_rows,
    vert_keys,
    vert_vals,
    vert_ids,
    vert_live,
    slash_keys,
    slash_vals,
    offsets,
    slash_live,
    block_index,
):
    head_width = q_rows.shape[-1]
    score_scale = head_width ** (-0.5)
    positions = jnp.arange(q_rows.shape[0], dtype=jnp.int32)
    causal = positions[None, :] <= positions[:, None]
    vert_scores = (
        jnp.einsum("qd,skd->qsk", q_rows, vert_keys, preferred_element_type=jnp.float32)
        * score_scale
    )
    slash_scores = (
        jnp.einsum("qd,nkd->qnk", q_rows, slash_keys, preferred_element_type=jnp.float32)
        * score_scale
    )
    distance = block_index - vert_ids
    on_slash = jnp.any((distance[:, None] == offsets[None, :]) & slash_live[None, :], axis=1)
    vert_ok = vert_live & (vert_ids >= 0) & (vert_ids <= block_index) & jnp.logical_not(on_slash)
    vert_mask = vert_ok[None, :, None] & (
        (vert_ids < block_index)[None, :, None] | causal[:, None, :]
    )
    slash_ok = slash_live & (block_index - offsets >= 0)
    slash_mask = slash_ok[None, :, None] & ((offsets > 0)[None, :, None] | causal[:, None, :])
    vert_scores = jnp.where(vert_mask, vert_scores, -jnp.inf)
    slash_scores = jnp.where(slash_mask, slash_scores, -jnp.inf)
    row_max = jnp.maximum(jnp.max(vert_scores, axis=(1, 2)), jnp.max(slash_scores, axis=(1, 2)))
    vert_exp = jnp.exp(vert_scores - row_max[:, None, None])
    slash_exp = jnp.exp(slash_scores - row_max[:, None, None])
    row_total = jnp.sum(vert_exp, axis=(1, 2)) + jnp.sum(slash_exp, axis=(1, 2))
    vert_weight = (vert_exp / row_total[:, None, None]).astype(jnp.bfloat16)
    slash_weight = (slash_exp / row_total[:, None, None]).astype(jnp.bfloat16)
    result = jnp.einsum("qsk,skd->qd", vert_weight, vert_vals, preferred_element_type=jnp.float32)
    result = result + jnp.einsum(
        "qnk,nkd->qd", slash_weight, slash_vals, preferred_element_type=jnp.float32
    )
    return result.astype(jnp.bfloat16)


def group_order(counts, group_count):
    group_size = H // group_count
    ranking = jnp.argsort(counts * H + jnp.arange(H, dtype=jnp.int32), stable=True)
    index = jnp.arange(H, dtype=jnp.int32)
    group = index // group_size
    within = index % group_size
    rank_of = within * group_count + jnp.where(within % 2 == 0, group, group_count - 1 - group)
    return ranking[rank_of]


def body(queries, key_values, gate_logits, vertical_blocks, slash_offsets, slash_count):
    group_count = lax.axis_size("head")
    seq_rank = lax.axis_index("seq")
    group_rank = lax.axis_index("head")
    group_size = H // group_count
    tok_rows = queries.shape[0]
    tok_dev = tok_rows * group_count
    blocks_dev = tok_dev // BLOCK
    head_slot = group_order(slash_count, group_count)
    kv_index = head_slot // (H // KVH)
    my_heads = lax.dynamic_slice_in_dim(head_slot, group_rank * group_size, group_size)
    q_grouped = jnp.take(queries.reshape(tok_rows, H, DH), head_slot, axis=1)
    my_queries = lax.all_to_all(q_grouped, "head", split_axis=1, concat_axis=0, tiled=True)
    whole_pairs = lax.all_gather(key_values, "head", axis=0, tiled=True)
    my_kv = lax.dynamic_slice_in_dim(kv_index, group_rank * group_size, group_size)
    my_pairs = jnp.take(whole_pairs.reshape(tok_dev, 2, KVH, DH), my_kv, axis=2)
    earlier = []
    for distance in range(REACH, 0, -1):
        earlier.append(from_behind(my_pairs, "seq", distance))
    reach_keys = jnp.concatenate(earlier + [my_pairs], axis=0)
    reach_blocks = reach_keys.reshape((REACH + 1) * blocks_dev, BLOCK, 2, group_size, DH)
    pair_blocks = my_pairs.reshape(blocks_dev, BLOCK, 2, group_size, DH)
    my_vertical = jnp.take(vertical_blocks, my_heads, axis=0)
    owned = my_vertical // blocks_dev == seq_rank
    block_range = jnp.arange(blocks_dev, dtype=jnp.int32)
    owned_ids = jnp.max(jnp.where(owned, my_vertical, -1), axis=1)
    local_block = owned_ids - seq_rank * blocks_dev
    selector = ((local_block[:, None] == block_range[None, :]) & (owned_ids >= 0)[:, None]).astype(
        jnp.bfloat16
    )
    packed = jnp.einsum(
        "pt,tbxpd->pxbd", selector, pair_blocks, preferred_element_type=jnp.float32
    ).astype(jnp.bfloat16)
    vert_data, vert_all_ids = (
        lax.all_gather(packed[None], "seq", axis=0, tiled=True),
        lax.all_gather(owned_ids[None], "seq", axis=0, tiled=True),
    )

    def vertical_for(head_pos):
        chosen = lax.dynamic_index_in_dim(vert_data, head_pos, 1, keepdims=False)
        chosen_ids = lax.dynamic_index_in_dim(vert_all_ids, head_pos, 1, keepdims=False)
        return (chosen[:, 0], chosen[:, 1], chosen_ids, jnp.ones(chosen_ids.shape, dtype=bool))

    slot_range_ns = jnp.arange(NS, dtype=jnp.int32)
    my_offsets = jnp.take(slash_offsets, my_heads, axis=0)
    my_counts = jnp.take(slash_count, my_heads, axis=0)

    def head_pass(head_pos):
        vert_keys, vert_vals, vert_ids, vert_live = vertical_for(head_pos)
        head_queries = lax.dynamic_index_in_dim(my_queries, head_pos, 1, keepdims=False).reshape(
            blocks_dev, BLOCK, DH
        )
        head_reach = lax.dynamic_index_in_dim(reach_blocks, head_pos, 3, keepdims=False)
        offsets = lax.dynamic_index_in_dim(my_offsets, head_pos, 0, keepdims=False)
        slash_live = slot_range_ns < lax.dynamic_index_in_dim(
            my_counts, head_pos, 0, keepdims=False
        )

        def query_pass(inputs):
            q_rows, local_index = inputs
            block_index = seq_rank * blocks_dev + local_index
            slash_index = REACH * blocks_dev + local_index - offsets
            slash_blocks = jnp.take(head_reach, slash_index, axis=0)
            return block_attend(
                q_rows,
                vert_keys,
                vert_vals,
                vert_ids,
                vert_live,
                slash_blocks[:, :, 0],
                slash_blocks[:, :, 1],
                offsets,
                slash_live,
                block_index,
            )

        return lax.map(query_pass, (head_queries, block_range))

    attended = lax.map(head_pass, jnp.arange(group_size, dtype=jnp.int32)).reshape(
        group_size, tok_dev, DH
    )
    returned = lax.all_to_all(attended, "head", split_axis=1, concat_axis=0, tiled=True)
    head_range_all = jnp.arange(H, dtype=jnp.int32)
    inverse = jnp.sum(
        jnp.where(head_slot[None, :] == head_range_all[:, None], head_range_all[None, :], 0), axis=1
    )
    natural = jnp.take(returned, inverse, axis=0)
    gate = jax.nn.sigmoid(gate_logits.astype(jnp.float32)).reshape(tok_rows, H, DH)
    gated = gate * jnp.transpose(natural, (1, 0, 2)).astype(jnp.float32)
    return gated.astype(jnp.bfloat16).reshape(tok_rows, H * DH)


def solution(mesh):
    in_specs = (
        P(("seq", "head"), None),
        P(("seq", "head"), None, None),
        P(("seq", "head"), None),
        P(),
        P(),
        P(),
    )
    out_specs = P(("seq", "head"), None)
    return jax.shard_map(body, mesh=mesh, in_specs=in_specs, out_specs=out_specs, check_vma=False)
```

profile of v0, /device:TPU:1, one launch (start us, length us, event | category | flops | bytes accessed | tf_op | source)
XLA Modules:
  0.0 331.5 jit_solution(11809386844297845460)
XLA Ops:
  12.1 32.1 %all-gather.5.cloned.1.call-done = bf16[256,2,1024]{2,1,0:T(2,128)(2,1)} async-done(((bf16[32,2,1024]{2,1,0:T(2,128)(2,1)}), bf16[256,2,1024]{2,1,0:T(2,128)(2,1)}) %all-gather.5.cloned.1.call-update) | async-done | bytes 1048592 | tf_op jit(solution)/shard_map/all_gather | solution.py:90
  44.1 2.4 copy.60
  50.7 3.6 %all-to-all-start = ((bf16[32,32,128]{2,0,1:T(8,128)(2,1)}), bf16[32,32,128]{2,0,1:T(8,128)(2,1)S(1)}, u32[]{:S(2)}, u32[]{:S(2)}) async-start(bf16[32,32,128]{2,0,1:T(8,128)(2,1)} %select_bitcast_fusion), calls=%async_computation | async-start | bytes 524288 | tf_op jit(solution)/shard_map/all_to_all | solution.py:89
  55.1 4.2 %collective-permute-start = (bf16[256,2,4,128]{3,0,1,2:T(8,128)(2,1)S(1)}, bf16[256,2,4,128]{3,0,1,2:T(8,128)(2,1)S(1)}, u32[]{:S(2)}, u32[]{:S(2)}) collective-permute-start(bf16[256,2,4,128]{3,0,1,2:T(8,128)(2,1)S(1)} %bitcast_select_fusion), channel_id=1, source_target_pairs={{0,16},{8,24},{16,32},{24,40},{32,48},{40,56},{48,64},{56,72},{64,... | collective-permute-start | bytes 1572872 | tf_op jit(solution)/shard_map/ppermute | solution.py:17
  59.3 3.3 collective-permute-start.1
  64.9 45.2 %all-reduce = s32[256]{0:T(256)S(1)} all-reduce(s32[256]{0:T(256)S(1)} %dynamic-update-slice), channel_id=3, replica_groups=mesh['seq'=64,'head'=8] {'seq'}, use_global_device_ids=true, to_apply=%add | all-reduce | flops 256 | bytes 2048
  112.4 60.5 %all-gather.7.cloned.1.call-done = bf16[256,2,64,128]{3,2,1,0:T(8,128)(2,1)} async-done(((bf16[4,2,64,128]{3,2,1,0:T(8,128)(2,1)}), bf16[256,2,64,128]{3,2,1,0:T(8,128)(2,1)}) %all-gather.7.cloned.1.call-update) | async-done | bytes 8388624 | tf_op jit(solution)/shard_map/all_gather | solution.py:111
  172.9 136.7 %while.37 = (s32[]{:T(128)}, bf16[4,4,64,128]{3,2,1,0:T(8,128)(2,1)}, s32[4]{0:T(128)S(1)}, bf16[256,4,128]{2,0,1:T(8,128)(2,1)S(1)}, s32[4,8]{1,0:T(4,128)S(1)}...) while((s32[]{:T(128)}, ...), condition=%wide.region_11.12_spmd.clone.clone, body=%wide.region_3.11_spmd.clone.clone.sunk | while | flops 154098576 | bytes 21907556 | solution.py:155
  180.7 25.7 %while.38 = (s32[]{:T(128)}, bf16[4,64,128]{2,1,0:T(8,128)(2,1)S(1)}, s32[64]{0:T(128)S(1)}, s32[4]{0:T(128)S(1)}, s32[]{:T(128)}, /*index=5*/s32[8]{0:T(128)S(1...) while((s32[]{:T(128)}, ...), condition=%wide.region_10.10_spmd, body=%wide.region_4.9_spmd.sunk | while | flops 154098560 | bytes 12468941 | solution.py:153
  182.1 1.9 fusion.56
  188.5 1.9 fusion.56
  201.4 1.9 fusion.56
  214.9 25.7 %while.38 = (s32[]{:T(128)}, bf16[4,64,128]{2,1,0:T(8,128)(2,1)S(1)}, s32[64]{0:T(128)S(1)}, s32[4]{0:T(128)S(1)}, s32[]{:T(128)}, /*index=5*/s32[8]{0:T(128)S(1...) while((s32[]{:T(128)}, ...), condition=%wide.region_10.10_spmd, body=%wide.region_4.9_spmd.sunk | while | flops 154098560 | bytes 12468941 | solution.py:153
  216.2 1.9 fusion.56
  222.7 1.9 fusion.56
  235.5 1.9 fusion.56
  249.0 25.7 %while.38 = (s32[]{:T(128)}, bf16[4,64,128]{2,1,0:T(8,128)(2,1)S(1)}, s32[64]{0:T(128)S(1)}, s32[4]{0:T(128)S(1)}, s32[]{:T(128)}, /*index=5*/s32[8]{0:T(128)S(1...) while((s32[]{:T(128)}, ...), condition=%wide.region_10.10_spmd, body=%wide.region_4.9_spmd.sunk | while | flops 154098560 | bytes 12468941 | solution.py:153
  250.4 1.9 fusion.56
  256.8 1.9 fusion.56
  263.3 1.9 fusion.56
  269.7 1.9 fusion.56
  283.2 25.7 %while.38 = (s32[]{:T(128)}, bf16[4,64,128]{2,1,0:T(8,128)(2,1)S(1)}, s32[64]{0:T(128)S(1)}, s32[4]{0:T(128)S(1)}, s32[]{:T(128)}, /*index=5*/s32[8]{0:T(128)S(1...) while((s32[]{:T(128)}, ...), condition=%wide.region_10.10_spmd, body=%wide.region_4.9_spmd.sunk | while | flops 154098560 | bytes 12468941 | solution.py:153
  311.5 5.2 %all-to-all-start.1 = ((bf16[4,256,128]{2,0,1:T(4,128)(2,1)}), bf16[4,256,128]{2,0,1:T(4,128)(2,1)S(1)}, u32[]{:S(2)}, u32[]{:S(2)}) async-start(bf16[4,256,128]{2,0,1:T(4,128)(2,1)} %bitcast.26), calls=%async_computation.1 | async-start | bytes 524288 | tf_op jit(solution)/shard_map/all_to_all | solution.py:158
  316.7 6.4 %all-to-all-done.1 = bf16[4,256,128]{2,0,1:T(4,128)(2,1)S(1)} async-done(((bf16[4,256,128]{2,0,1:T(4,128)(2,1)}), bf16[4,256,128]{2,0,1:T(4,128)(2,1)S(1)}, u32[]{:S(2)}, u32[]{:S(2)}) %all-to-all-start.1) | async-done | bytes 262176 | tf_op jit(solution)/shard_map/all_to_all | solution.py:158
  (420 shorter events, 107.2 us)
Async XLA Ops:
  6.5 42.7 %copy-start = (bf16[32,4096]{1,0:T(8,128)(2,1)S(1)}, bf16[32,4096]{1,0:T(8,128)(2,1)}, u32[]{:S(2)}) copy-start(bf16[32,4096]{1,0:T(8,128)(2,1)} %param.10) | copy-start | bytes 786436
  6.5 37.6 %all-gather.5.cloned.1.call-start = ((), (), s32[]{:S(2)}) async-start(), calls=%async_computation.2 | async-start | bytes 1179648 | tf_op jit(solution)/shard_map/all_gather | solution.py:90
  7.3 165.6 %all-gather.7.cloned.1.call-start = ((), (), s32[]{:S(2)}) async-start(), calls=%async_computation.3 | async-start | bytes 8519680 | tf_op jit(solution)/shard_map/all_gather | solution.py:111
  48.0 6.3 %copy-start.1 = (s32[32]{0:T(128)S(1)}, s32[32]{0:T(128)}, u32[]{:S(2)}) copy-start(s32[32]{0:T(128)} %param.15) | copy-start | bytes 388
  48.5 61.8 %copy-start.4 = (s32[32,8]{0,1:T(8,128)S(1)}, s32[32,8]{0,1:T(8,128)}, u32[]{:S(2)}) copy-start(s32[32,8]{0,1:T(8,128)} %param.14) | copy-start | bytes 3076
  50.7 60.3 %all-to-all-start = ((bf16[32,32,128]{2,0,1:T(8,128)(2,1)}), bf16[32,32,128]{2,0,1:T(8,128)(2,1)S(1)}, u32[]{:S(2)}, u32[]{:S(2)}) async-start(bf16[32,32,128]{2,0,1:T(8,128)(2,1)} %select_bitcast_fusion), calls=%async_computation | async-start | bytes 524288 | tf_op jit(solution)/shard_map/all_to_all | solution.py:89
  55.1 55.9 %collective-permute-start = (bf16[256,2,4,128]{3,0,1,2:T(8,128)(2,1)S(1)}, bf16[256,2,4,128]{3,0,1,2:T(8,128)(2,1)S(1)}, u32[]{:S(2)}, u32[]{:S(2)}) collective-permute-start(bf16[256,2,4,128]{3,0,1,2:T(8,128)(2,1)S(1)} %bitcast_select_fusion), channel_id=1, source_target_pairs={{0,16},{8,24},{16,32},{24,40},{32,48},{40,56},{48,64},{56,72},{64,... | collective-permute-start | bytes 1572872 | tf_op jit(solution)/shard_map/ppermute | solution.py:17
  59.3 51.7 %collective-permute-start.1 = (bf16[256,2,4,128]{3,0,1,2:T(8,128)(2,1)S(1)}, bf16[256,2,4,128]{3,0,1,2:T(8,128)(2,1)S(1)}, u32[]{:S(2)}, u32[]{:S(2)}) collective-permute-start(bf16[256,2,4,128]{3,0,1,2:T(8,128)(2,1)S(1)} %bitcast_select_fusion), channel_id=1, source_target_pairs={{0,8},{8,16},{16,24},{24,32},{32,40},{40,48},{48,56},{56,64},{64,7... | collective-permute-start | bytes 1572872 | tf_op jit(solution)/shard_map/ppermute | solution.py:17
  185.4 1.2 copy-start.2
  191.8 1.2 copy-start.2
  198.2 1.2 copy-start.2
  204.7 1.2 copy-start.2
  219.5 1.2 copy-start.2
  226.0 1.2 copy-start.2
  232.4 1.2 copy-start.2
  238.8 1.2 copy-start.2
  253.7 1.2 copy-start.2
  260.2 1.2 copy-start.2
  266.6 1.2 copy-start.2
  273.0 1.2 copy-start.2
  287.9 1.2 copy-start.2
  294.3 1.2 copy-start.2
  309.6 14.2 %copy-start.3 = (bf16[32,4096]{1,0:T(8,128)(2,1)S(1)}, bf16[32,4096]{1,0:T(8,128)(2,1)}, u32[]{:S(2)}) copy-start(bf16[32,4096]{1,0:T(8,128)(2,1)} %param.12) | copy-start | bytes 786436
  311.5 11.6 %all-to-all-start.1 = ((bf16[4,256,128]{2,0,1:T(4,128)(2,1)}), bf16[4,256,128]{2,0,1:T(4,128)(2,1)S(1)}, u32[]{:S(2)}, u32[]{:S(2)}) async-start(bf16[4,256,128]{2,0,1:T(4,128)(2,1)} %bitcast.26), calls=%async_computation.1 | async-start | bytes 524288 | tf_op jit(solution)/shard_map/all_to_all | solution.py:158
  (2 other events, 2.5 us)
Sparse Core Ops, SparseCore 0:
  9.5 34.5 all-gather.4
  49.3 123.5 all-gather.6
where the time goes:
time: 334 us; the launch traced here: 332 us
  waiting for transfers between devices  99.8 us (30%)
  local copies, waits for them, and re-layouts  57.9 us (17%)
  matrix products  47.2 us (14%)
  blocking collectives  45.2 us (14%)
  loops' own time  27.9 us (8%)
  other arithmetic  23.1 us (7%)
  starting transfers between devices  16.3 us (5%)
  between operations  14.3 us (4%)
    all_gather x1, waiting for transfers between devices, body(): lax.all_gather(packed[None], 'seq', axis=0, tiled=True)  60.5 us
    unnamed x1, blocking collectives  45.2 us
    all_gather x1, waiting for transfers between devices, body(): whole_pairs = lax.all_gather(key_values, 'head', axis=0, tiled=True)  32.1 us
    dot_general x16, matrix products, block_attend(): jnp.einsum('qd,skd->qsk', q_rows, vert_keys, preferred_element_type=jnp.f...  30.9 us
    another operation x4, loops' own time, head_pass(): return lax.map(query_pass, (head_queries, block_range))  21 us
    dynamic_slice x20, local copies, waits for them, and re-layouts, body(): lax.map(head_pass, jnp.arange(group_size, dtype=jnp.int32))  12.1 us
    reduce_sum x32, other arithmetic, block_attend(): row_total = jnp.sum(vert_exp, axis=(1, 2)) + jnp.sum(slash_exp, axis=(1, 2))  10.5 us
    gather x16, local copies, waits for them, and re-layouts, query_pass(): slash_blocks = jnp.take(head_reach, slash_index, axis=0)  9.56 us
  transfers between devices with their start and end apart: 6, of which 3 were waited for; matrix products, arithmetic and copies ran while one was open for 3% of the time, Pallas kernels for 0%

commit v1 on v0

v1 whole, which is shorter than its diff:
```python
import jax
import jax.numpy as jnp
from jax import lax
from jax.experimental import pallas as pl
from jax.experimental.pallas import tpu as pltpu
from jax.sharding import Mesh
from jax.sharding import PartitionSpec as P

H = 32
KVH = 8
DH = 128
BLOCK = 64
NV = 16
NS = 8
ROWS = 32
LO = 16
HI = 32
GROUP = 4
LOWEST = -3.0e38
EXP2_SCALE = DH**-0.5 * 1.4426950408889634

VERT, QDYN, QNAT, KVNAT, IN_ROWS = 0, 64, 192, 256, 320
OV, OS, STATS, OUT_ROWS = 0, 128, 192, 224
SLOTS = GROUP + 2
L_LANE = 64
M_HEAD, M_SLOT, M_MASK, M_KV, M_HI, M_LO, M_LEN = 0, 32, 64, 96, 104, 105, 106

bf16 = jnp.bfloat16
f32 = jnp.float32
SMEM = pl.BlockSpec(memory_space=pltpu.SMEM)
VMEM = pl.BlockSpec(memory_space=pltpu.VMEM)


def tables(vertical_blocks, slash_offsets, slash_count):
    hi = lax.axis_index("hi")
    lo = lax.axis_index("lo")
    heads = jnp.arange(H, dtype=jnp.int32)
    groups = H // GROUP
    order = slash_count * H + heads
    rank = jnp.sum((order[None, :] < order[:, None]).astype(jnp.int32), axis=1)
    within = rank // groups
    place = rank % groups
    group = jnp.where(within % 2 == 0, place, groups - 1 - place)
    slot = group * GROUP + within
    head_of = jnp.sum(jnp.where(slot[None, :] == heads[:, None], heads[None, :], 0), axis=1)
    live = jnp.arange(NS, dtype=jnp.int32)[None, :] < slash_count[:, None]
    mask = jnp.sum(jnp.where(live, jnp.left_shift(1, slash_offsets), 0), axis=1)
    shard = hi * 2 + lo // (LO // 2)
    here = jnp.any(vertical_blocks // 4 == shard, axis=1)
    kv_of = jnp.sum(
        jnp.where(
            (group[None, :] == jnp.arange(groups, dtype=jnp.int32)[:, None]) & here[None, :],
            (heads // (H // KVH))[None, :],
            0,
        ),
        axis=1,
    )
    return jnp.concatenate([head_of, slot, mask, kv_of, jnp.stack([hi, lo])]).astype(jnp.int32)


def entry_kernel(meta, q_ref, kv_ref, out_ref):
    def q_cols(head):
        return q_ref[:, pl.ds(pl.multiple_of(head * DH, DH), DH)]

    def kv_cols(which, head):
        return kv_ref[:, pl.ds(pl.multiple_of(which * KVH * DH + head * DH, DH), DH)]

    for g in range(KVH):
        kv_head = meta[M_KV + g]
        parts = [kv_cols(0, kv_head), kv_cols(1, kv_head)]
        parts += [q_cols(meta[M_HEAD + g * GROUP + p]) for p in range(GROUP)]
        tail = [kv_cols(0, g), kv_cols(1, g)]
        for c in range(2):
            own = [q_cols(4 * g + 2 * c), q_cols(4 * g + 2 * c + 1)]
            for n, part in enumerate(parts + own + tail):
                out_ref[2 * g + c, n * ROWS : (n + 1) * ROWS, :] = part


def pick_kernel(meta, vert_ref, in_ref, spread_ref, kv_ref):
    lo = meta[M_LO]
    g = lo >> 1
    c = lo & 1
    shard = meta[M_HI] * 2 + c
    block = jnp.int32(0)
    for p in range(GROUP):
        head = meta[M_HEAD + g * GROUP + p]
        for j in range(NV):
            v = vert_ref[head, j]
            block = jnp.where((v >> 2) == shard, v & 3, block)
    first = c * (LO // 2) + 2 * block
    for half in range(2):
        for which in range(2):
            part = in_ref[first + half, VERT + which * ROWS : VERT + (which + 1) * ROWS, :]
            at = which * BLOCK + half * ROWS
            for d in range(HI):
                spread_ref[d, at : at + ROWS, :] = part
    kv_ref[...] = in_ref[:, KVNAT:, :]


def split(x, pieces):
    out = []
    for _ in range(pieces - 1):
        top = x.astype(bf16).astype(f32)
        out.append(top)
        x = x - top
    return out + [x]


def stats_tile(slot, row_max, row_sum, lane, base):
    for n, part in enumerate(split(row_max, 3)):
        base = jnp.where(lane == 3 * slot + n, part, base)
    for n, part in enumerate(split(row_sum, 2)):
        base = jnp.where(lane == L_LANE + 2 * slot + n, part, base)
    return base


def scores(q, k):
    return lax.dot_general(q, k, (((1,), (1,)), ((), ())), preferred_element_type=f32)


def slash_kernel(meta, in_ref, before_ref, out_ref, stats_ref, k_buf, v_buf):
    half = LO * ROWS
    k_buf[0:half, :] = before_ref[:, 0:ROWS, :].reshape(half, DH)
    v_buf[0:half, :] = before_ref[:, ROWS : 2 * ROWS, :].reshape(half, DH)
    k_buf[half:, :] = in_ref[:, KVNAT : KVNAT + ROWS, :].reshape(half, DH)
    v_buf[half:, :] = in_ref[:, KVNAT + ROWS : KVNAT + 2 * ROWS, :].reshape(half, DH)
    lo = meta[M_LO]
    first_block = meta[M_HI] * 8
    band = 8 * BLOCK
    offset = 8 - lax.broadcasted_iota(jnp.int32, (1, band), 1) // BLOCK
    causal = jnp.where(
        lax.broadcasted_iota(jnp.int32, (BLOCK, BLOCK), 1)
        <= lax.broadcasted_iota(jnp.int32, (BLOCK, BLOCK), 0),
        0.0,
        -jnp.inf,
    )
    lane = lax.broadcasted_iota(jnp.int32, (BLOCK, DH), 1)
    live = []
    for a in range(2):
        mask = meta[M_MASK + 2 * lo + a]
        live.append((jnp.right_shift(jnp.full((1, band), mask, jnp.int32), offset) & 1) == 1)
    for i in range(8):
        at = i * BLOCK
        reach = offset <= first_block + i
        q = jnp.concatenate(
            [
                in_ref[2 * i : 2 * i + 2, QNAT + a * ROWS : QNAT + (a + 1) * ROWS, :].reshape(
                    BLOCK, DH
                )
                for a in range(2)
            ],
            axis=0,
        )
        far = scores(q, k_buf[at : at + band, :])
        near = scores(q, k_buf[at + band : at + band + BLOCK, :])
        tile = jnp.zeros((BLOCK, DH), f32)
        for a in range(2):
            rows = slice(a * BLOCK, (a + 1) * BLOCK)
            s_far = far[rows] + jnp.where(live[a] & reach, 0.0, -jnp.inf)
            s_near = near[rows] + causal
            top = jnp.maximum(
                jnp.max(s_far, axis=1, keepdims=True), jnp.max(s_near, axis=1, keepdims=True)
            )
            e_far = jnp.exp2((s_far - top) * EXP2_SCALE)
            e_near = jnp.exp2((s_near - top) * EXP2_SCALE)
            total = jnp.sum(e_far, axis=1, keepdims=True) + jnp.sum(e_near, axis=1, keepdims=True)
            acc = jnp.dot(
                e_far.astype(bf16), v_buf[at : at + band, :], preferred_element_type=f32
            ) + jnp.dot(
                e_near.astype(bf16),
                v_buf[at + band : at + band + BLOCK, :],
                preferred_element_type=f32,
            )
            out_ref[2 * i : 2 * i + 2, a * ROWS : (a + 1) * ROWS, :] = acc.astype(bf16).reshape(
                2, ROWS, DH
            )
            tile = stats_tile(GROUP + a, top, total, lane, tile)
        stats_ref[2 * i : 2 * i + 2] = tile.astype(bf16).reshape(2, ROWS, DH)


def vertical_kernel(
    meta, vert_ref, in_ref, all_ref, slash_ref, slash_stats_ref, out_ref, k_buf, v_buf
):
    lo = meta[M_LO]
    g = lo >> 1
    c = lo & 1
    first_block = meta[M_HI] * 8
    width = NV * BLOCK
    out_ref[:, OS:STATS, :] = slash_ref[...]
    out_ref[:, STATS:, :] = slash_stats_ref[...]
    of_lane = lax.broadcasted_iota(jnp.int32, (1, width), 1) // BLOCK
    for p in range(GROUP):
        head = meta[M_HEAD + g * GROUP + p]
        count = jnp.int32(0)
        ids = jnp.full((1, width), 1 << 20, jnp.int32)
        for j in range(NV):
            k_buf[j * BLOCK : (j + 1) * BLOCK, :] = jnp.zeros((BLOCK, DH), bf16)
            v_buf[j * BLOCK : (j + 1) * BLOCK, :] = jnp.zeros((BLOCK, DH), bf16)
        for j in range(NV):
            v = vert_ref[head, j]
            mine = ((v >> 2) & 1) == c
            source = v >> 3
            at = pl.multiple_of(count * BLOCK, BLOCK)

            @pl.when(mine)
            def _():
                k_buf[pl.ds(at, BLOCK), :] = all_ref[source, 0:BLOCK, :]
                v_buf[pl.ds(at, BLOCK), :] = all_ref[source, BLOCK : 2 * BLOCK, :]

            ids = jnp.where(mine & (of_lane == count), v, ids)
            count = count + mine.astype(jnp.int32)
        mask = jnp.full((1, width), meta[M_MASK + head], jnp.int32)

        def attend(n):
            size = n * BLOCK
            k_all = k_buf[0:size, :]
            v_all = v_buf[0:size, :]
            lane = lax.broadcasted_iota(jnp.int32, (2 * BLOCK, DH), 1)
            for i in range(4):
                q = in_ref[
                    4 * i : 4 * i + 4, QDYN + p * ROWS : QDYN + (p + 1) * ROWS, :
                ].reshape(2 * BLOCK, DH)
                s = scores(q, k_all)
                parts = []
                for t in range(2):
                    distance = first_block + 2 * i + t - ids[:, 0:size]
                    slashed = jnp.right_shift(mask[:, 0:size], jnp.clip(distance, 0, 31)) & 1
                    bias = jnp.where((distance > 0) & (slashed == 0), 0.0, -jnp.inf)
                    parts.append(s[t * BLOCK : (t + 1) * BLOCK] + bias)
                s = jnp.concatenate(parts, axis=0)
                top = jnp.maximum(jnp.max(s, axis=1, keepdims=True), LOWEST)
                e = jnp.exp2((s - top) * EXP2_SCALE)
                total = jnp.sum(e, axis=1, keepdims=True)
                acc = jnp.dot(e.astype(bf16), v_all, preferred_element_type=f32)
                out_ref[4 * i : 4 * i + 4, OV + p * ROWS : OV + (p + 1) * ROWS, :] = acc.astype(
                    bf16
                ).reshape(4, ROWS, DH)
                base = out_ref[4 * i : 4 * i + 4, STATS:, :].reshape(2 * BLOCK, DH).astype(f32)
                tile = stats_tile(p, top, total, lane, base)
                out_ref[4 * i : 4 * i + 4, STATS:, :] = tile.astype(bf16).reshape(4, ROWS, DH)

        for low, n in ((0, 8), (8, 12), (12, 16)):

            @pl.when((count > low if low else count >= 0) & (count <= n))
            def _(n=n):
                attend(n)


def exit_kernel(meta, in_ref, gate_ref, out_ref, m_buf, l_buf):
    row = lax.broadcasted_iota(jnp.int32, (DH, SLOTS * DH), 0)
    col = lax.broadcasted_iota(jnp.int32, (DH, SLOTS * DH), 1) // DH
    m_pick = jnp.where((row >= 3 * col) & (row < 3 * col + 3), 1.0, 0.0).astype(bf16)
    l_at = row - L_LANE
    l_pick = jnp.where((l_at >= 2 * col) & (l_at < 2 * col + 2), 1.0, 0.0).astype(bf16)
    stats = in_ref[:, STATS:, :].reshape(LO * ROWS, DH)
    m_buf[...] = jnp.dot(stats, m_pick, preferred_element_type=f32).reshape(
        LO, ROWS, SLOTS * DH
    )
    l_buf[...] = jnp.dot(stats, l_pick, preferred_element_type=f32).reshape(
        LO, ROWS, SLOTS * DH
    )
    for h in range(H):
        source = h // 2
        a = h % 2
        cols = slice((GROUP + a) * DH, (GROUP + a + 1) * DH)
        tops = [m_buf[source, :, cols]]
        sums = [l_buf[source, :, cols]]
        accs = [in_ref[source, OS + a * ROWS : OS + (a + 1) * ROWS, :]]
        slot = meta[M_SLOT + h]
        p = slot & 3
        lanes = pl.ds(pl.multiple_of(p * DH, DH), DH)
        for c in range(2):
            source = 2 * (slot >> 2) + c
            tops.append(m_buf[source, :, lanes])
            sums.append(l_buf[source, :, lanes])
            accs.append(in_ref[source, pl.ds(pl.multiple_of(OV + p * ROWS, ROWS), ROWS), :])
        best = jnp.maximum(jnp.maximum(tops[0], tops[1]), tops[2])
        num = jnp.zeros((ROWS, DH), f32)
        den = jnp.zeros((ROWS, DH), f32)
        for top, total, acc in zip(tops, sums, accs):
            w = jnp.exp2((top - best) * EXP2_SCALE)
            num = num + w * acc.astype(f32)
            den = den + w * total
        attended = (num / den).astype(bf16).astype(f32)
        gate = gate_ref[:, h * DH : (h + 1) * DH].astype(f32)
        out_ref[:, h * DH : (h + 1) * DH] = (jax.nn.sigmoid(gate) * attended).astype(bf16)


def call(kernel, out_shape, in_specs, scratch=(), name=None):
    return pl.pallas_call(
        kernel,
        out_shape=out_shape,
        in_specs=in_specs,
        out_specs=jax.tree.map(lambda _: VMEM, out_shape),
        scratch_shapes=list(scratch),
        name=name,
    )


def body(queries, key_values, gate_logits, vertical_blocks, slash_offsets, slash_count):
    meta = tables(vertical_blocks, slash_offsets, slash_count)
    flat_kv = key_values.reshape(ROWS, 2 * KVH * DH)
    sent = call(
        entry_kernel,
        jax.ShapeDtypeStruct((LO, IN_ROWS, DH), bf16),
        [SMEM, VMEM, VMEM],
        name="entry",
    )(meta, queries, flat_kv)
    mine = lax.all_to_all(sent, "lo", 0, 0, tiled=True)
    spread, kv_own = call(
        pick_kernel,
        (
            jax.ShapeDtypeStruct((HI, 2 * BLOCK, DH), bf16),
            jax.ShapeDtypeStruct((LO, 2 * ROWS, DH), bf16),
        ),
        [SMEM, SMEM, VMEM],
        name="pick",
    )(meta, vertical_blocks, mine)
    verticals = lax.all_to_all(spread, "hi", 0, 0, tiled=True)
    kv_before = lax.ppermute(kv_own, "hi", [(i, i + 1) for i in range(HI - 1)])
    slash, slash_stats = call(
        slash_kernel,
        (
            jax.ShapeDtypeStruct((LO, 2 * ROWS, DH), bf16),
            jax.ShapeDtypeStruct((LO, ROWS, DH), bf16),
        ),
        [SMEM, VMEM, VMEM],
        [pltpu.VMEM((2 * LO * ROWS, DH), bf16)] * 2,
        name="slash",
    )(meta, mine, kv_before)
    partial = call(
        vertical_kernel,
        jax.ShapeDtypeStruct((LO, OUT_ROWS, DH), bf16),
        [SMEM, SMEM, VMEM, VMEM, VMEM, VMEM],
        [pltpu.VMEM((NV * BLOCK, DH), bf16)] * 2,
        name="vertical",
    )(meta, vertical_blocks, mine, verticals, slash, slash_stats)
    back = lax.all_to_all(partial, "lo", 0, 0, tiled=True)
    return call(
        exit_kernel,
        jax.ShapeDtypeStruct((ROWS, H * DH), bf16),
        [SMEM, VMEM, VMEM],
        [pltpu.VMEM((LO, ROWS, SLOTS * DH), f32)] * 2,
        name="exit",
    )(meta, back, gate_logits)


def solution(mesh):
    pairs = Mesh(mesh.devices.reshape(HI, LO), ("hi", "lo"))
    tokens = P(("hi", "lo"))
    return jax.shard_map(
        body,
        mesh=pairs,
        in_specs=(tokens, tokens, tokens, P(), P(), P()),
        out_specs=tokens,
        check_vma=False,
    )
```

time: 334 us -> 130 us (0.39)
  the two profiles are of different devices: /device:TPU:1 before, /device:TPU:8 now
where the time goes in v1:
time: 130 us; the launch traced here: 129 us
  waiting for transfers between devices  52.9 us (41%)
  starting transfers between devices  26 us (20%)
  Pallas kernels  21.7 us (17%)
  blocking collectives  20.2 us (16%)
  local copies, waits for them, and re-layouts  5.71 us (4%)
  other arithmetic  2.52 us (2%)
    ppermute x1, waiting for transfers between devices, body(): kv_before = lax.ppermute(kv_own, 'hi', [(i, i + 1) for i in range(HI - 1)])  34.2 us
    all_to_all x1, blocking collectives, body(): back = lax.all_to_all(partial, 'lo', 0, 0, tiled=True)  20.2 us
    all_to_all x1, waiting for transfers between devices, body(): mine = lax.all_to_all(sent, 'lo', 0, 0, tiled=True)  18.7 us
    all_to_all x1, starting transfers between devices, body(): verticals = lax.all_to_all(spread, 'hi', 0, 0, tiled=True)  15.4 us
    pallas_call x1, Pallas kernels, body(): call(vertical_kernel, jax.ShapeDtypeStruct((LO, OUT_ROWS, DH), bf16), [SM...  8.83 us
    all_to_all x1, starting transfers between devices, body(): mine = lax.all_to_all(sent, 'lo', 0, 0, tiled=True)  6.34 us
    unnamed x12, local copies, waits for them, and re-layouts  5.03 us
    pallas_call x1, Pallas kernels, body(): call(slash_kernel, (jax.ShapeDtypeStruct((LO, 2 * ROWS, DH), bf16), jax.S...  4.93 us
  transfers between devices with their start and end apart: 3, of which 2 were waited for; matrix products, arithmetic and copies ran while one was open for 1% of the time, Pallas kernels for 4%

profile of v1, /device:TPU:8, one launch (start us, length us, event | category | flops | bytes accessed | tf_op | source)
XLA Modules:
  0.0 129.1 jit_solution(17420573468669519010)
XLA Ops:
  0.0 0.7 iota_add_fusion
  0.7 0.7 select_reduce_fusion.2
  1.4 0.2 convert_reduce_fusion
  1.6 0.1 select_reduce_fusion
  1.7 1.6 %copy.11 = bf16[4,8,2,1024]{3,1,2,0:T(8,128)(2,1)} copy(bf16[4,8,2,1024]{3,2,1,0:T(2,128)(2,1)} %bitcast.5) | data formatting | bytes 262144
  3.3 0.7 fusion.3
  4.0 0.1 select_reduce_fusion.1
  4.1 0.7 concatenate.3.meta
  4.8 2.3 %entry.1 = bf16[16,320,128]{2,1,0:T(8,128)(2,1)} custom-call(s32[106]{0:T(128)} %concatenate.3.meta, bf16[32,4096]{1,0:T(8,128)(2,1)} %q_ref.1, bf16[32,2048]{1,0:T(8,128)(2,1)} %bitcast.4), custom_call_target="tpu_custom_call" | custom-call | tf_op jit(solution)/shard_map/entry/pallas_call | solution.py:303
  7.1 6.3 %all-to-all-start = ((bf16[16,320,128]{2,1,0:T(8,128)(2,1)}), bf16[16,320,128]{2,1,0:T(8,128)(2,1)S(1)}, u32[]{:S(2)}, u32[]{:S(2)}) async-start(bf16[16,320,128]{2,1,0:T(8,128)(2,1)} %entry.1), calls=%async_computation | async-start | bytes 2621440 | tf_op jit(solution)/shard_map/all_to_all | solution.py:309
  13.4 0.7 copy.10.vert_ref
  14.1 18.7 %all-to-all-done.in_ref = bf16[16,320,128]{2,1,0:T(8,128)(2,1)S(1)} async-done(((bf16[16,320,128]{2,1,0:T(8,128)(2,1)}), bf16[16,320,128]{2,1,0:T(8,128)(2,1)S(1)}, u32[]{:S(2)}, u32[]{:S(2)}) %all-to-all-start) | async-done | bytes 1310752 | tf_op jit(solution)/shard_map/all_to_all | solution.py:309
  32.8 1.1 copy-done
  33.9 2.7 %pick.1 = (bf16[32,128,128]{2,1,0:T(8,128)(2,1)}, bf16[16,64,128]{2,1,0:T(8,128)(2,1)}) custom-call(s32[106]{0:T(128)} %concatenate.3.meta, s32[32,16]{1,0:T(8,128)} %copy.10.vert_ref, bf16[16,320,128]{2,1,0:T(8,128)(2,1)} %copy-done), custom_call_target="tpu_custom_call" | custom-call | tf_op jit(solution)/shard_map/pick/pallas_call | solution.py:310
  36.5 15.4 %all-to-all-start.1 = ((bf16[32,128,128]{2,1,0:T(8,128)(2,1)}), bf16[32,128,128]{2,1,0:T(8,128)(2,1)S(1)}, u32[]{:S(2)}, u32[]{:S(2)}) async-start(bf16[32,128,128]{2,1,0:T(8,128)(2,1)} %get-tuple-element.9), calls=%async_computation.1 | async-start | bytes 2097152 | tf_op jit(solution)/shard_map/all_to_all | solution.py:319
  52.0 4.3 %collective-permute-start = (bf16[16,64,128]{2,1,0:T(8,128)(2,1)S(1)}, bf16[16,64,128]{2,1,0:T(8,128)(2,1)S(1)}, u32[]{:S(2)}, u32[]{:S(2)}) collective-permute-start(bf16[16,64,128]{2,1,0:T(8,128)(2,1)S(1)} %copy-done.4), channel_id=1, source_target_pairs={{0,16},{16,32},{32,48},{48,64},{64,80},{80,96},{96,112},{112,128},... | collective-permute-start | bytes 786440 | tf_op jit(solution)/shard_map/ppermute | solution.py:320
  56.2 34.2 %collective-permute-done.before_ref = bf16[16,64,128]{2,1,0:T(8,128)(2,1)S(1)} collective-permute-done((bf16[16,64,128]{2,1,0:T(8,128)(2,1)S(1)}, bf16[16,64,128]{2,1,0:T(8,128)(2,1)S(1)}, u32[]{:S(2)}, u32[]{:S(2)}) %collective-permute-start) | collective-permute-done | bytes 262176 | tf_op jit(solution)/shard_map/ppermute | solution.py:320
  90.5 0.7 copy-done.2
  91.2 4.9 %slash.1 = (bf16[16,64,128]{2,1,0:T(8,128)(2,1)}, bf16[16,32,128]{2,1,0:T(8,128)(2,1)}) custom-call(s32[106]{0:T(128)} %concatenate.3.meta, bf16[16,320,128]{2,1,0:T(8,128)(2,1)} %copy-done, bf16[16,64,128]{2,1,0:T(8,128)(2,1)} %copy-done.2), custom_call_target="tpu_custom_call" | custom-call | tf_op jit(solution)/shard_map/slash/pallas_call | solution.py:321
  96.1 0.0 all-to-all-done.1.all_ref
  96.1 1.0 copy-done.1
  97.1 8.8 %vertical.1 = bf16[16,224,128]{2,1,0:T(8,128)(2,1)} custom-call(s32[106]{0:T(128)} %concatenate.3.meta, s32[32,16]{1,0:T(8,128)} %copy.10.vert_ref, bf16[16,320,128]{2,1,0:T(8,128)(2,1)} %copy-done, bf16[32,128,128]{2,1,0:T(8,128)(2,1)} %copy-done.1, bf16[16,64,128]{2,1,0:T(8,128)(2,1)} %get-tuple-element.11.slash_ref, ...), custom_call_target="tpu_custom_call" | custom-call | tf_op jit(solution)/shard_map/vertical/pallas_call | solution.py:331
  105.9 20.2 %all_to_all.15.in_ref = bf16[16,224,128]{2,1,0:T(8,128)(2,1)} all-to-all(bf16[16,224,128]{2,1,0:T(8,128)(2,1)} %vertical.1), channel_id=1, replica_groups=mesh['seq'=64,'head'=8] {'seq':(32)2,'head'}, dimensions={0} | all-to-all | bytes 1835008 | tf_op jit(solution)/shard_map/all_to_all | solution.py:338
  126.1 3.0 %exit.1 = bf16[32,4096]{1,0:T(8,128)(2,1)} custom-call(s32[106]{0:T(128)} %concatenate.3.meta, bf16[16,224,128]{2,1,0:T(8,128)(2,1)} %all_to_all.15.in_ref, bf16[32,4096]{1,0:T(8,128)(2,1)} %gate_ref.1), custom_call_target="tpu_custom_call" | custom-call | tf_op jit(solution)/shard_map/exit/pallas_call | solution.py:339
  (8 shorter events, 0.0 us)
Async XLA Ops:
  7.1 6.4 %copy-start.3 = (s32[32,16]{0,1:T(8,128)S(1)}, s32[32,16]{0,1:T(8,128)}, u32[]{:S(2)}) copy-start(s32[32,16]{0,1:T(8,128)} %param.9) | copy-start | bytes 6148
  7.1 25.7 %all-to-all-start = ((bf16[16,320,128]{2,1,0:T(8,128)(2,1)}), bf16[16,320,128]{2,1,0:T(8,128)(2,1)S(1)}, u32[]{:S(2)}, u32[]{:S(2)}) async-start(bf16[16,320,128]{2,1,0:T(8,128)(2,1)} %entry.1), calls=%async_computation | async-start | bytes 2621440 | tf_op jit(solution)/shard_map/all_to_all | solution.py:309
  32.8 1.1 copy-start
  36.5 15.4 %copy-start.4 = (bf16[16,64,128]{2,1,0:T(8,128)(2,1)S(1)}, bf16[16,64,128]{2,1,0:T(8,128)(2,1)}, u32[]{:S(2)}) copy-start(bf16[16,64,128]{2,1,0:T(8,128)(2,1)} %get-tuple-element.10) | copy-start | bytes 786436
  36.5 59.6 %all-to-all-start.1 = ((bf16[32,128,128]{2,1,0:T(8,128)(2,1)}), bf16[32,128,128]{2,1,0:T(8,128)(2,1)S(1)}, u32[]{:S(2)}, u32[]{:S(2)}) async-start(bf16[32,128,128]{2,1,0:T(8,128)(2,1)} %get-tuple-element.9), calls=%async_computation.1 | async-start | bytes 2097152 | tf_op jit(solution)/shard_map/all_to_all | solution.py:319
  52.0 38.5 %collective-permute-start = (bf16[16,64,128]{2,1,0:T(8,128)(2,1)S(1)}, bf16[16,64,128]{2,1,0:T(8,128)(2,1)S(1)}, u32[]{:S(2)}, u32[]{:S(2)}) collective-permute-start(bf16[16,64,128]{2,1,0:T(8,128)(2,1)S(1)} %copy-done.4), channel_id=1, source_target_pairs={{0,16},{16,32},{32,48},{48,64},{64,80},{80,96},{96,112},{112,128},... | collective-permute-start | bytes 786440 | tf_op jit(solution)/shard_map/ppermute | solution.py:320
  90.5 0.7 copy-start.2
  96.1 1.0 copy-start.1

commit v2 on v1

v2 whole, which is shorter than its diff:
```python
import jax
import jax.numpy as jnp
from jax import lax
from jax.experimental import pallas as pl
from jax.experimental.pallas import tpu as pltpu
from jax.sharding import Mesh
from jax.sharding import PartitionSpec as P

H = 32
KVH = 8
DH = 128
BLOCK = 64
NV = 16
NS = 8
ROWS = 32
LO = 16
NY = 8
NK = 4
HI = NY * NK
GROUP = 4
LOWEST = -3.0e38
EXP2_SCALE = DH**-0.5 * 1.4426950408889634

VERT, QDYN, KVNAT, QNAT, IN_ROWS = 0, 64, 128, 160, 224
OV, OS, STATS, OUT_ROWS = 0, 128, 192, 224
SLOTS = GROUP + 2
L_LANE = 8
PART = 32
M_HEAD, M_SLOT, M_MASK, M_KV, M_HI, M_LO, M_LEN = 0, 32, 64, 96, 104, 105, 106

bf16 = jnp.bfloat16
f32 = jnp.float32
SMEM = pl.BlockSpec(memory_space=pltpu.SMEM)
VMEM = pl.BlockSpec(memory_space=pltpu.VMEM)


def tables(vertical_blocks, slash_offsets, slash_count):
    hi = lax.axis_index(("y", "k"))
    lo = lax.axis_index("lo")
    heads = jnp.arange(H, dtype=jnp.int32)
    groups = H // GROUP
    order = slash_count * H + heads
    rank = jnp.sum((order[None, :] < order[:, None]).astype(jnp.int32), axis=1)
    within = rank // groups
    place = rank % groups
    group = jnp.where(within % 2 == 0, place, groups - 1 - place)
    slot = group * GROUP + within
    head_of = jnp.sum(jnp.where(slot[None, :] == heads[:, None], heads[None, :], 0), axis=1)
    live = jnp.arange(NS, dtype=jnp.int32)[None, :] < slash_count[:, None]
    mask = jnp.sum(jnp.where(live, jnp.left_shift(1, slash_offsets), 0), axis=1)
    shard = hi * 2 + lo // (LO // 2)
    here = jnp.any(vertical_blocks // 4 == shard, axis=1)
    kv_of = jnp.sum(
        jnp.where(
            (group[None, :] == jnp.arange(groups, dtype=jnp.int32)[:, None]) & here[None, :],
            (heads // (H // KVH))[None, :],
            0,
        ),
        axis=1,
    )
    return jnp.concatenate([head_of, slot, mask, kv_of, jnp.stack([hi, lo])]).astype(jnp.int32)


def entry_kernel(meta, q_ref, kv_ref, out_ref):
    def q_cols(head):
        return q_ref[:, pl.ds(pl.multiple_of(head * DH, DH), DH)]

    def kv_cols(which, head):
        return kv_ref[:, pl.ds(pl.multiple_of(which * KVH * DH + head * DH, DH), DH)]

    for g in range(KVH):
        kv_head = meta[M_KV + g]
        vert = [kv_cols(0, kv_head), kv_cols(1, kv_head)]
        for c in range(2):
            parts = vert + [q_cols(meta[M_HEAD + g * GROUP + 2 * c + p]) for p in range(2)]
            parts += [kv_cols(c, g), q_cols(4 * g + 2 * c), q_cols(4 * g + 2 * c + 1)]
            for n, part in enumerate(parts):
                out_ref[2 * g + c, n * ROWS : (n + 1) * ROWS, :] = part


def pick_kernel(meta, vert_ref, in_ref, spread_ref, swap_ref, kv_ref):
    lo = meta[M_LO]
    g = lo >> 1
    c = lo & 1
    shard = meta[M_HI] * 2 + c
    block = jnp.int32(0)
    for p in range(GROUP):
        head = meta[M_HEAD + g * GROUP + p]
        for j in range(NV):
            v = vert_ref[head, j]
            block = jnp.where((v >> 2) == shard, v & 3, block)
    first = c * (LO // 2) + 2 * block
    for half in range(2):
        for which in range(2):
            part = in_ref[first + half, VERT + which * ROWS : VERT + (which + 1) * ROWS, :]
            at = which * BLOCK + half * ROWS
            for d in range(NK):
                spread_ref[d, at : at + ROWS, :] = part
    swap_ref[...] = in_ref[:, QDYN:QNAT, :]
    kv_ref[...] = in_ref[:, KVNAT:QNAT, :]


def scores(q, k):
    return lax.dot_general(q, k, (((1,), (1,)), ((), ())), preferred_element_type=f32)


def slash_kernel(meta, in_ref, swap_ref, before_ref, before_swap_ref, out_ref, stats_ref, k_buf, v_buf):
    half = LO * ROWS
    lo = meta[M_LO]
    for c in range(2):

        @pl.when((lo & 1) == c)
        def _(c=c):
            mine, other = (k_buf, v_buf) if c == 0 else (v_buf, k_buf)
            mine[0:half, :] = before_ref[...].reshape(half, DH)
            other[0:half, :] = before_swap_ref[...].reshape(half, DH)
            mine[half:, :] = in_ref[:, KVNAT:QNAT, :].reshape(half, DH)
            other[half:, :] = swap_ref[:, KVNAT - QDYN :, :].reshape(half, DH)

    first_block = meta[M_HI] * 8
    band = 8 * BLOCK
    offset = 8 - lax.broadcasted_iota(jnp.int32, (1, band), 1) // BLOCK
    causal = jnp.where(
        lax.broadcasted_iota(jnp.int32, (BLOCK, BLOCK), 1)
        <= lax.broadcasted_iota(jnp.int32, (BLOCK, BLOCK), 0),
        0.0,
        -jnp.inf,
    )
    lane = lax.broadcasted_iota(jnp.int32, (BLOCK, DH), 1)
    live = []
    for a in range(2):
        mask = meta[M_MASK + 2 * lo + a]
        live.append((jnp.right_shift(jnp.full((1, band), mask, jnp.int32), offset) & 1) == 1)

    def step(i, _):
        at = pl.multiple_of(i * BLOCK, BLOCK)
        near_at = pl.multiple_of(i * BLOCK + band, BLOCK)
        reach = offset <= first_block + i
        two = pl.ds(2 * i, 2)
        q = jnp.concatenate(
            [
                in_ref[two, QNAT + a * ROWS : QNAT + (a + 1) * ROWS, :].reshape(BLOCK, DH)
                for a in range(2)
            ],
            axis=0,
        )
        far = scores(q, k_buf[pl.ds(at, band), :])
        near = scores(q, k_buf[pl.ds(near_at, BLOCK), :])
        tile = jnp.zeros((BLOCK, DH), f32)
        for a in range(2):
            rows = slice(a * BLOCK, (a + 1) * BLOCK)
            s_far = far[rows] + jnp.where(live[a] & reach, 0.0, -jnp.inf)
            s_near = near[rows] + causal
            top = jnp.maximum(
                jnp.max(s_far, axis=1, keepdims=True), jnp.max(s_near, axis=1, keepdims=True)
            )
            e_far = jnp.exp2((s_far - top) * EXP2_SCALE)
            e_near = jnp.exp2((s_near - top) * EXP2_SCALE)
            total = jnp.sum(e_far, axis=1, keepdims=True) + jnp.sum(e_near, axis=1, keepdims=True)
            acc = jnp.dot(
                e_far.astype(bf16), v_buf[pl.ds(at, band), :], preferred_element_type=f32
            ) + jnp.dot(
                e_near.astype(bf16), v_buf[pl.ds(near_at, BLOCK), :], preferred_element_type=f32
            )
            out_ref[two, a * ROWS : (a + 1) * ROWS, :] = acc.astype(bf16).reshape(2, ROWS, DH)
            tile = jnp.where(lane == GROUP + a, top, tile)
            tile = jnp.where(lane == L_LANE + GROUP + a, total, tile)
        stats_ref[two] = tile.reshape(2, ROWS, DH)
        return 0

    lax.fori_loop(0, 8, step, 0)


def vertical_kernel(
    meta,
    vert_ref,
    in_ref,
    swap_ref,
    all_ref,
    slash_ref,
    slash_stats_ref,
    out_ref,
    q_buf,
    k_buf,
    v_buf,
    stats_buf,
):
    lo = meta[M_LO]
    g = lo >> 1
    c = lo & 1
    first_block = meta[M_HI] * 8
    tokens = LO * ROWS
    width = NV * BLOCK
    out_ref[:, OS:STATS, :] = slash_ref[...]
    stats_buf[...] = slash_stats_ref[...].reshape(tokens, DH)
    k_buf[...] = jnp.zeros(k_buf.shape, bf16)
    v_buf[...] = jnp.zeros(v_buf.shape, bf16)
    for t in range(2):
        rows = slice(t * ROWS, (t + 1) * ROWS)
        q_buf[2 * c + t] = in_ref[:, QDYN + t * ROWS : QDYN + (t + 1) * ROWS, :].reshape(tokens, DH)
        q_buf[2 * (1 - c) + t] = swap_ref[:, rows, :].reshape(tokens, DH)
    of_lane = lax.broadcasted_iota(jnp.int32, (1, width), 1) // BLOCK
    lane = lax.broadcasted_iota(jnp.int32, (2 * BLOCK, DH), 1)

    def head_step(p, _):
        head = meta[M_HEAD + g * GROUP + p]
        count = jnp.int32(0)
        ids = jnp.full((1, width), 1 << 20, jnp.int32)
        for j in range(NV):
            v = vert_ref[head, j]
            mine = ((v >> 2) & 1) == c
            source = v >> 3
            at = pl.multiple_of(count * BLOCK, BLOCK)
            k_buf[pl.ds(at, BLOCK), :] = all_ref[source, 0:BLOCK, :]
            v_buf[pl.ds(at, BLOCK), :] = all_ref[source, BLOCK : 2 * BLOCK, :]
            ids = jnp.where(of_lane == jnp.where(mine, count, NV), v, ids)
            count = count + mine.astype(jnp.int32)
        mask = jnp.full((1, width), meta[M_MASK + head], jnp.int32)

        def attend(n):
            size = n * BLOCK

            def step(i, _):
                at = pl.multiple_of(i * 2 * BLOCK, 2 * BLOCK)
                s = scores(q_buf[p, pl.ds(at, 2 * BLOCK), :], k_buf[0:size, :])
                parts = []
                for t in range(2):
                    distance = first_block + 2 * i + t - ids[:, 0:size]
                    slashed = jnp.right_shift(mask[:, 0:size], jnp.clip(distance, 0, 31)) & 1
                    bias = jnp.where((distance > 0) & (slashed == 0), 0.0, -jnp.inf)
                    parts.append(s[t * BLOCK : (t + 1) * BLOCK] + bias)
                s = jnp.concatenate(parts, axis=0)
                top = jnp.maximum(jnp.max(s, axis=1, keepdims=True), LOWEST)
                e = jnp.exp2((s - top) * EXP2_SCALE)
                total = jnp.sum(e, axis=1, keepdims=True)
                acc = jnp.dot(e.astype(bf16), v_buf[0:size, :], preferred_element_type=f32)
                rows = pl.ds(pl.multiple_of(OV + p * ROWS, ROWS), ROWS)
                out_ref[pl.ds(4 * i, 4), rows, :] = acc.astype(bf16).reshape(4, ROWS, DH)
                tile = stats_buf[pl.ds(at, 2 * BLOCK), :]
                tile = jnp.where(lane == p, top, tile)
                stats_buf[pl.ds(at, 2 * BLOCK), :] = jnp.where(lane == L_LANE + p, total, tile)
                return 0

            lax.fori_loop(0, 4, step, 0)

        for low, n in ((-1, 8), (8, 12), (12, 16)):

            @pl.when((count > low) & (count <= n))
            def _(n=n):
                attend(n)

        return 0

    lax.fori_loop(0, GROUP, head_step, 0)
    stats = stats_buf[...]
    first = stats.astype(bf16).astype(f32)
    stats = stats - first
    second = stats.astype(bf16).astype(f32)
    third = stats - second
    packed = first + pltpu.roll(second, PART, 1) + pltpu.roll(third, 2 * PART, 1)
    out_ref[:, STATS:, :] = packed.astype(bf16).reshape(LO, ROWS, DH)


def exit_kernel(meta, in_ref, gate_ref, out_ref, m_buf, l_buf):
    row = lax.broadcasted_iota(jnp.int32, (DH, SLOTS * DH), 0)
    col = lax.broadcasted_iota(jnp.int32, (DH, SLOTS * DH), 1) // DH
    row = jnp.where(row < 3 * PART, row % PART, PART)
    m_pick = jnp.where(row == col, 1.0, 0.0).astype(bf16)
    l_pick = jnp.where(row == col + L_LANE, 1.0, 0.0).astype(bf16)
    stats = in_ref[:, STATS:, :].reshape(LO * ROWS, DH)
    m_buf[...] = jnp.dot(stats, m_pick, preferred_element_type=f32).reshape(LO, ROWS, SLOTS * DH)
    l_buf[...] = jnp.dot(stats, l_pick, preferred_element_type=f32).reshape(LO, ROWS, SLOTS * DH)

    def source_step(n, _):
        for a in range(2):
            h = 2 * n + a
            cols = slice((GROUP + a) * DH, (GROUP + a + 1) * DH)
            tops = [m_buf[n, :, cols]]
            sums = [l_buf[n, :, cols]]
            accs = [in_ref[n, OS + a * ROWS : OS + (a + 1) * ROWS, :]]
            slot = meta[M_SLOT + h]
            p = slot & 3
            lanes = pl.ds(pl.multiple_of(p * DH, DH), DH)
            for c in range(2):
                source = 2 * (slot >> 2) + c
                tops.append(m_buf[source, :, lanes])
                sums.append(l_buf[source, :, lanes])
                accs.append(in_ref[source, pl.ds(pl.multiple_of(OV + p * ROWS, ROWS), ROWS), :])
            best = jnp.maximum(jnp.maximum(tops[0], tops[1]), tops[2])
            num = jnp.zeros((ROWS, DH), f32)
            den = jnp.zeros((ROWS, DH), f32)
            for top, total, acc in zip(tops, sums, accs):
                w = jnp.exp2((top - best) * EXP2_SCALE)
                num = num + w * acc.astype(f32)
                den = den + w * total
            attended = (num / den).astype(bf16).astype(f32)
            at = pl.ds(pl.multiple_of(h * DH, DH), DH)
            gate = gate_ref[:, at].astype(f32)
            out_ref[:, at] = (jax.nn.sigmoid(gate) * attended).astype(bf16)
        return 0

    lax.fori_loop(0, LO, source_step, 0, unroll=2)


def call(kernel, out_shape, in_specs, scratch=(), name=None):
    return pl.pallas_call(
        kernel,
        out_shape=out_shape,
        in_specs=in_specs,
        out_specs=jax.tree.map(lambda _: VMEM, out_shape),
        scratch_shapes=list(scratch),
        name=name,
    )


def shape(rows, dtype=bf16, lead=LO):
    return jax.ShapeDtypeStruct((lead, rows, DH), dtype)


def body(queries, key_values, gate_logits, vertical_blocks, slash_offsets, slash_count):
    meta = tables(vertical_blocks, slash_offsets, slash_count)
    flat_kv = key_values.reshape(ROWS, 2 * KVH * DH)
    sent = call(entry_kernel, shape(IN_ROWS), [SMEM, VMEM, VMEM], name="entry")(
        meta, queries, flat_kv
    )
    mine = lax.all_to_all(sent, "lo", 0, 0, tiled=True)
    spread, swap, kv_own = call(
        pick_kernel,
        (shape(2 * BLOCK, lead=NK), shape(QNAT - QDYN), shape(ROWS)),
        [SMEM, SMEM, VMEM],
        name="pick",
    )(meta, vertical_blocks, mine)
    row = lax.all_to_all(spread, "k", 0, 0, tiled=True).reshape(1, NK * 2 * BLOCK, DH)
    spread_row = jnp.broadcast_to(row, (NY, NK * 2 * BLOCK, DH))
    verticals = lax.all_to_all(spread_row, "y", 0, 0, tiled=True).reshape(HI, 2 * BLOCK, DH)
    partner = [(i, i ^ 1) for i in range(LO)]
    swapped = lax.ppermute(swap, "lo", partner)
    before = lax.ppermute(kv_own, ("y", "k"), [(i, i + 1) for i in range(HI - 1)])
    before_swap = lax.ppermute(before, "lo", partner)
    slash, slash_stats = call(
        slash_kernel,
        (shape(2 * ROWS), shape(ROWS, f32)),
        [SMEM, VMEM, VMEM, VMEM, VMEM],
        [pltpu.VMEM((2 * LO * ROWS, DH), bf16)] * 2,
        name="slash",
    )(meta, mine, swapped, before, before_swap)
    partial = call(
        vertical_kernel,
        shape(OUT_ROWS),
        [SMEM, SMEM, VMEM, VMEM, VMEM, VMEM, VMEM],
        [
            pltpu.VMEM((GROUP, LO * ROWS, DH), bf16),
            pltpu.VMEM(((NV + 1) * BLOCK, DH), bf16),
            pltpu.VMEM(((NV + 1) * BLOCK, DH), bf16),
            pltpu.VMEM((LO * ROWS, DH), f32),
        ],
        name="vertical",
    )(meta, vertical_blocks, mine, swapped, verticals, slash, slash_stats)
    back = lax.all_to_all(partial, "lo", 0, 0, tiled=True)
    return call(
        exit_kernel,
        jax.ShapeDtypeStruct((ROWS, H * DH), bf16),
        [SMEM, VMEM, VMEM],
        [pltpu.VMEM((LO, ROWS, SLOTS * DH), f32)] * 2,
        name="exit",
    )(meta, back, gate_logits)


def solution(mesh):
    pairs = Mesh(mesh.devices.reshape(NY, NK, LO), ("y", "k", "lo"))
    tokens = P(("y", "k", "lo"))
    return jax.shard_map(
        body,
        mesh=pairs,
        in_specs=(tokens, tokens, tokens, P(), P(), P()),
        out_specs=tokens,
        check_vma=False,
    )
```

time: 130 us -> 131 us (level)
  the two profiles are of different devices: /device:TPU:8 before, /device:TPU:40 now
where the time goes in v2:
time: 131 us; the launch traced here: 130 us
  blocking collectives  38.5 us (29%)
  waiting for transfers between devices  37.9 us (29%)
  Pallas kernels  24.1 us (18%)
  starting transfers between devices  19.9 us (15%)
  local copies, waits for them, and re-layouts  9.14 us (7%)
    ppermute x1, waiting for transfers between devices, body(): lax.ppermute(kv_own, ('y', 'k'), [(i, i + 1) for i in range(HI - 1)])  22.1 us
    all_to_all x1, blocking collectives, body(): back = lax.all_to_all(partial, 'lo', 0, 0, tiled=True)  20.2 us
    all_to_all x1, blocking collectives, body(): lax.all_to_all(spread, 'k', 0, 0, tiled=True).reshape(1, NK * 2 * BLOCK, DH)  18.3 us
    all_to_all x1, waiting for transfers between devices, body(): mine = lax.all_to_all(sent, 'lo', 0, 0, tiled=True)  14.5 us
    pallas_call x1, Pallas kernels, body(): call(vertical_kernel, shape(OUT_ROWS), [SMEM, SMEM, VMEM, VMEM, VMEM, VME...  10.8 us
    unnamed x22, local copies, waits for them, and re-layouts  7.35 us
    all_to_all x1, starting transfers between devices, body(): lax.all_to_all(spread_row, 'y', 0, 0, tiled=True).reshape(HI, 2 * BLOCK, DH)  7.22 us
    all_to_all x1, starting transfers between devices, body(): mine = lax.all_to_all(sent, 'lo', 0, 0, tiled=True)  6.21 us
  transfers between devices with their start and end apart: 5, of which 3 were waited for; matrix products, arithmetic and copies ran while one was open for 1% of the time, Pallas kernels for 5%

profile of v2, /device:TPU:40, one launch (start us, length us, event | category | flops | bytes accessed | tf_op | source)
XLA Modules:
  0.0 130.2 jit_solution(10524279703589474234)
XLA Ops:
  0.0 0.7 copy-done.7
  1.4 1.6 %copy.11 = bf16[4,8,2,1024]{3,1,2,0:T(8,128)(2,1)} copy(bf16[4,8,2,1024]{3,2,1,0:T(2,128)(2,1)} %bitcast.9) | data formatting | bytes 262144
  3.0 0.7 copy-done.5
  3.8 0.7 concatenate.3.meta
  4.5 2.1 %entry.1 = bf16[16,224,128]{2,1,0:T(8,128)(2,1)} custom-call(s32[106]{0:T(128)} %concatenate.3.meta, bf16[32,4096]{1,0:T(8,128)(2,1)} %q_ref.1, bf16[32,2048]{1,0:T(8,128)(2,1)} %bitcast.7), custom_call_target="tpu_custom_call" | custom-call | tf_op jit(solution)/shard_map/entry/pallas_call | solution.py:323
  6.6 6.2 %all-to-all-start = ((bf16[16,224,128]{2,1,0:T(8,128)(2,1)}), bf16[16,224,128]{2,1,0:T(8,128)(2,1)S(1)}, u32[]{:S(2)}, u32[]{:S(2)}) async-start(bf16[16,224,128]{2,1,0:T(8,128)(2,1)} %entry.1), calls=%async_computation | async-start | bytes 1835008 | tf_op jit(solution)/shard_map/all_to_all | solution.py:326
  12.8 0.7 copy.10.vert_ref
  13.5 14.5 %all-to-all-done.in_ref = bf16[16,224,128]{2,1,0:T(8,128)(2,1)S(1)} async-done(((bf16[16,224,128]{2,1,0:T(8,128)(2,1)}), bf16[16,224,128]{2,1,0:T(8,128)(2,1)S(1)}, u32[]{:S(2)}, u32[]{:S(2)}) %all-to-all-start) | async-done | bytes 917536 | tf_op jit(solution)/shard_map/all_to_all | solution.py:326
  27.9 1.0 copy-done
  28.9 2.1 %pick.1 = (bf16[4,128,128]{2,1,0:T(8,128)(2,1)}, bf16[16,96,128]{2,1,0:T(8,128)(2,1)}, bf16[16,32,128]{2,1,0:T(8,128)(2,1)}) custom-call(s32[106]{0:T(128)} %concatenate.3.meta, s32[32,16]{1,0:T(8,128)} %copy.10.vert_ref, bf16[16,224,128]{2,1,0:T(8,128)(2,1)} %copy-done), custom_call_target="tpu_custom_call" | custom-call | tf_op jit(solution)/shard_map/pick/pallas_call | solution.py:327
  31.0 18.3 %all_to_all.20 = bf16[4,128,128]{2,1,0:T(8,128)(2,1)S(1)} all-to-all(bf16[4,128,128]{2,1,0:T(8,128)(2,1)} %get-tuple-element.11), channel_id=1, replica_groups=mesh['y'=8,'k'=4,'lo'=16] {'k'}, dimensions={0} | all-to-all | bytes 262144 | tf_op jit(solution)/shard_map/all_to_all | solution.py:333
  49.3 1.1 broadcast_in_dim.52
  50.5 7.2 %all-to-all-start.2 = ((bf16[8,512,128]{2,1,0:T(8,128)(2,1)}), bf16[8,512,128]{2,1,0:T(8,128)(2,1)S(1)}, u32[]{:S(2)}, u32[]{:S(2)}) async-start(bf16[8,512,128]{2,1,0:T(8,128)(2,1)} %broadcast_in_dim.52), calls=%async_computation.2 | async-start | bytes 2097152 | tf_op jit(solution)/shard_map/all_to_all | solution.py:335
  57.7 1.9 %collective-permute-start = (bf16[16,96,128]{2,1,0:T(8,128)(2,1)S(1)}, bf16[16,96,128]{2,1,0:T(8,128)(2,1)S(1)}, u32[]{:S(2)}, u32[]{:S(2)}) collective-permute-start(bf16[16,96,128]{2,1,0:T(8,128)(2,1)S(1)} %copy-done.8), channel_id=1, source_target_pairs={{0,1},{1,0},{2,3},{3,2},{4,5},{5,4},{6,7},{7,6},{8,9},{9,8},{10,11... | collective-permute-start | bytes 1179656 | tf_op jit(solution)/shard_map/ppermute | solution.py:337
  59.6 2.6 %collective-permute-start.1 = (bf16[16,32,128]{2,1,0:T(8,128)(2,1)S(1)}, bf16[16,32,128]{2,1,0:T(8,128)(2,1)S(1)}, u32[]{:S(2)}, u32[]{:S(2)}) collective-permute-start(bf16[16,32,128]{2,1,0:T(8,128)(2,1)S(1)} %copy-done.9), channel_id=1, source_target_pairs={{0,16},{16,32},{32,48},{48,64},{64,80},{80,96},{96,112},{112,128},... | collective-permute-start | bytes 393224 | tf_op jit(solution)/shard_map/ppermute | solution.py:338
  62.3 22.1 %collective-permute-done.1.before_ref = bf16[16,32,128]{2,1,0:T(8,128)(2,1)S(1)} collective-permute-done((bf16[16,32,128]{2,1,0:T(8,128)(2,1)S(1)}, bf16[16,32,128]{2,1,0:T(8,128)(2,1)S(1)}, u32[]{:S(2)}, u32[]{:S(2)}) %collective-permute-start.1) | collective-permute-done | bytes 131104 | tf_op jit(solution)/shard_map/ppermute | solution.py:338
  84.4 1.9 %collective-permute-start.2 = (bf16[16,32,128]{2,1,0:T(8,128)(2,1)S(1)}, bf16[16,32,128]{2,1,0:T(8,128)(2,1)S(1)}, u32[]{:S(2)}, u32[]{:S(2)}) collective-permute-start(bf16[16,32,128]{2,1,0:T(8,128)(2,1)S(1)} %collective-permute-done.1.before_ref), channel_id=1, source_target_pairs={{0,1},{1,0},{2,3},{3,2},{4,5},{5,4},{6,7},{7,6},{8,9},{9,8},{10,11... | collective-permute-start | bytes 393224 | tf_op jit(solution)/shard_map/ppermute | solution.py:339
  86.3 1.3 %collective-permute-done.2.before_swap_ref = bf16[16,32,128]{2,1,0:T(8,128)(2,1)S(1)} collective-permute-done((bf16[16,32,128]{2,1,0:T(8,128)(2,1)S(1)}, bf16[16,32,128]{2,1,0:T(8,128)(2,1)S(1)}, u32[]{:S(2)}, u32[]{:S(2)}) %collective-permute-start.2) | collective-permute-done | bytes 131104 | tf_op jit(solution)/shard_map/ppermute | solution.py:339
  88.3 0.8 copy-done.2
  89.0 5.9 %slash.1 = (bf16[16,64,128]{2,1,0:T(8,128)(2,1)}, f32[16,32,128]{2,1,0:T(8,128)}) custom-call(s32[106]{0:T(128)} %concatenate.3.meta, bf16[16,224,128]{2,1,0:T(8,128)(2,1)} %copy-done, bf16[16,96,128]{2,1,0:T(8,128)(2,1)} %copy-done.2, bf16[16,32,128]{2,1,0:T(8,128)(2,1)} %copy-done.3, bf16[16,32,128]{2,1,0:T(8,128)(2,1)} %copy-done.4), custom_call_target="tpu_custom_call" | custom-call | tf_op jit(solution)/shard_map/slash/pallas_call | solution.py:340
  95.0 1.0 copy-done.1
  95.9 10.8 %vertical.1 = bf16[16,224,128]{2,1,0:T(8,128)(2,1)} custom-call(s32[106]{0:T(128)} %concatenate.3.meta, s32[32,16]{1,0:T(8,128)} %copy.10.vert_ref, bf16[16,224,128]{2,1,0:T(8,128)(2,1)} %copy-done, bf16[16,96,128]{2,1,0:T(8,128)(2,1)} %copy-done.2, bf16[32,128,128]{2,1,0:T(8,128)(2,1)} %bitcast.6, bf16[16,64,128]{2,1,0:T(8,128)(2,1)} %get-tuple-element.13.slash_ref, ...), custom_call_target="tpu_custom_call" | custom-call | tf_op jit(solution)/shard_map/vertical/pallas_call | solution.py:347
  106.7 20.2 %all_to_all.21.in_ref = bf16[16,224,128]{2,1,0:T(8,128)(2,1)} all-to-all(bf16[16,224,128]{2,1,0:T(8,128)(2,1)} %vertical.1), channel_id=1, replica_groups=mesh['y'=8,'k'=4,'lo'=16] {'lo'}, dimensions={0} | all-to-all | bytes 1835008 | tf_op jit(solution)/shard_map/all_to_all | solution.py:359
  126.9 3.3 %exit.1 = bf16[32,4096]{1,0:T(8,128)(2,1)} custom-call(s32[106]{0:T(128)} %concatenate.3.meta, bf16[16,224,128]{2,1,0:T(8,128)(2,1)} %all_to_all.21.in_ref, bf16[32,4096]{1,0:T(8,128)(2,1)} %gate_ref.1), custom_call_target="tpu_custom_call" | custom-call | tf_op jit(solution)/shard_map/exit/pallas_call | solution.py:360
  (24 shorter events, 1.5 us)
Async XLA Ops:
  0.0 0.7 copy-start.7
  0.7 0.7 copy-start.6
  3.0 0.7 copy-start.5
  6.6 21.4 %all-to-all-start = ((bf16[16,224,128]{2,1,0:T(8,128)(2,1)}), bf16[16,224,128]{2,1,0:T(8,128)(2,1)S(1)}, u32[]{:S(2)}, u32[]{:S(2)}) async-start(bf16[16,224,128]{2,1,0:T(8,128)(2,1)} %entry.1), calls=%async_computation | async-start | bytes 1835008 | tf_op jit(solution)/shard_map/all_to_all | solution.py:326
  27.9 1.0 copy-start
  50.5 7.2 %copy-start.8 = (bf16[16,96,128]{2,1,0:T(8,128)(2,1)S(1)}, bf16[16,96,128]{2,1,0:T(8,128)(2,1)}, u32[]{:S(2)}) copy-start(bf16[16,96,128]{2,1,0:T(8,128)(2,1)} %get-tuple-element.10) | copy-start | bytes 1179652
  50.5 9.1 %copy-start.9 = (bf16[16,32,128]{2,1,0:T(8,128)(2,1)S(1)}, bf16[16,32,128]{2,1,0:T(8,128)(2,1)}, u32[]{:S(2)}) copy-start(bf16[16,32,128]{2,1,0:T(8,128)(2,1)} %get-tuple-element.12) | copy-start | bytes 393220
  50.5 44.5 %all-to-all-start.2 = ((bf16[8,512,128]{2,1,0:T(8,128)(2,1)}), bf16[8,512,128]{2,1,0:T(8,128)(2,1)S(1)}, u32[]{:S(2)}, u32[]{:S(2)}) async-start(bf16[8,512,128]{2,1,0:T(8,128)(2,1)} %broadcast_in_dim.52), calls=%async_computation.2 | async-start | bytes 2097152 | tf_op jit(solution)/shard_map/all_to_all | solution.py:335
  57.7 29.9 %collective-permute-start = (bf16[16,96,128]{2,1,0:T(8,128)(2,1)S(1)}, bf16[16,96,128]{2,1,0:T(8,128)(2,1)S(1)}, u32[]{:S(2)}, u32[]{:S(2)}) collective-permute-start(bf16[16,96,128]{2,1,0:T(8,128)(2,1)S(1)} %copy-done.8), channel_id=1, source_target_pairs={{0,1},{1,0},{2,3},{3,2},{4,5},{5,4},{6,7},{7,6},{8,9},{9,8},{10,11... | collective-permute-start | bytes 1179656 | tf_op jit(solution)/shard_map/ppermute | solution.py:337
  59.6 24.8 %collective-permute-start.1 = (bf16[16,32,128]{2,1,0:T(8,128)(2,1)S(1)}, bf16[16,32,128]{2,1,0:T(8,128)(2,1)S(1)}, u32[]{:S(2)}, u32[]{:S(2)}) collective-permute-start(bf16[16,32,128]{2,1,0:T(8,128)(2,1)S(1)} %copy-done.9), channel_id=1, source_target_pairs={{0,16},{16,32},{32,48},{48,64},{64,80},{80,96},{96,112},{112,128},... | collective-permute-start | bytes 393224 | tf_op jit(solution)/shard_map/ppermute | solution.py:338
  84.4 3.2 %copy-start.3 = (bf16[16,32,128]{2,1,0:T(8,128)(2,1)}, bf16[16,32,128]{2,1,0:T(8,128)(2,1)S(1)}, u32[]{:S(2)}) copy-start(bf16[16,32,128]{2,1,0:T(8,128)(2,1)S(1)} %collective-permute-done.1.before_ref) | copy-start | bytes 393220
  84.4 3.2 %collective-permute-start.2 = (bf16[16,32,128]{2,1,0:T(8,128)(2,1)S(1)}, bf16[16,32,128]{2,1,0:T(8,128)(2,1)S(1)}, u32[]{:S(2)}, u32[]{:S(2)}) collective-permute-start(bf16[16,32,128]{2,1,0:T(8,128)(2,1)S(1)} %collective-permute-done.1.before_ref), channel_id=1, source_target_pairs={{0,1},{1,0},{2,3},{3,2},{4,5},{5,4},{6,7},{7,6},{8,9},{9,8},{10,11... | collective-permute-start | bytes 393224 | tf_op jit(solution)/shard_map/ppermute | solution.py:339
  87.6 0.7 copy-start.4
  88.3 0.8 copy-start.2
  95.0 1.0 copy-start.1

commit v3 on v2

--- a/solution.py
+++ b/solution.py
@@ -32,6 +32,7 @@
 f32 = jnp.float32
 SMEM = pl.BlockSpec(memory_space=pltpu.SMEM)
 VMEM = pl.BlockSpec(memory_space=pltpu.VMEM)
+LOADED = pl.BlockSpec(memory_space=pltpu.VMEM)
 
 
 def tables(vertical_blocks, slash_offsets, slash_count):
@@ -104,9 +105,16 @@
     return lax.dot_general(q, k, (((1,), (1,)), ((), ())), preferred_element_type=f32)
 
 
-def slash_kernel(meta, in_ref, swap_ref, before_ref, before_swap_ref, out_ref, stats_ref, k_buf, v_buf):
+def slash_kernel(
+    meta, in_ref, swap_ref, before_ref, before_swap_ref, out_ref, stats_ref, q_ref, k_buf, v_buf
+):
     half = LO * ROWS
     lo = meta[M_LO]
+    core = lo & 1
+    for t in range(2):
+        rows = slice(t * ROWS, (t + 1) * ROWS)
+        q_ref[2 * core + t] = in_ref[:, QDYN + t * ROWS : QDYN + (t + 1) * ROWS, :].reshape(half, DH)
+        q_ref[2 * (1 - core) + t] = swap_ref[:, rows, :].reshape(half, DH)
     for c in range(2):
 
         @pl.when((lo & 1) == c)
@@ -174,13 +182,11 @@
 def vertical_kernel(
     meta,
     vert_ref,
-    in_ref,
-    swap_ref,
+    q_buf,
     all_ref,
     slash_ref,
     slash_stats_ref,
     out_ref,
-    q_buf,
     k_buf,
     v_buf,
     stats_buf,
@@ -195,10 +201,6 @@
     stats_buf[...] = slash_stats_ref[...].reshape(tokens, DH)
     k_buf[...] = jnp.zeros(k_buf.shape, bf16)
     v_buf[...] = jnp.zeros(v_buf.shape, bf16)
-    for t in range(2):
-        rows = slice(t * ROWS, (t + 1) * ROWS)
-        q_buf[2 * c + t] = in_ref[:, QDYN + t * ROWS : QDYN + (t + 1) * ROWS, :].reshape(tokens, DH)
-        q_buf[2 * (1 - c) + t] = swap_ref[:, rows, :].reshape(tokens, DH)
     of_lane = lax.broadcasted_iota(jnp.int32, (1, width), 1) // BLOCK
     lane = lax.broadcasted_iota(jnp.int32, (2 * BLOCK, DH), 1)
 
@@ -302,19 +304,34 @@
     lax.fori_loop(0, LO, source_step, 0, unroll=2)
 
 
-def call(kernel, out_shape, in_specs, scratch=(), name=None):
-    return pl.pallas_call(
+def call(kernel, out_shape, in_specs, scratch=(), name=None, **options):
+    run = pl.pallas_call(
         kernel,
         out_shape=out_shape,
         in_specs=in_specs,
-        out_specs=jax.tree.map(lambda _: VMEM, out_shape),
+        out_specs=tuple(VMEM for _ in out_shape) if isinstance(out_shape, tuple) else VMEM,
         scratch_shapes=list(scratch),
         name=name,
-    )
+        **options,
+    )
+
+    def placed(*args):
+        return run(
+            *(
+                pltpu.with_memory_space_constraint(arg, pltpu.VMEM) if spec is VMEM else arg
+                for arg, spec in zip(args, in_specs)
+            )
+        )
+
+    return placed
 
 
 def shape(rows, dtype=bf16, lead=LO):
     return jax.ShapeDtypeStruct((lead, rows, DH), dtype)
+
+
+def in_vmem(rows, lead=LO):
+    return pltpu.VMEM((lead, rows, DH), bf16)
 
 
 def body(queries, key_values, gate_logits, vertical_blocks, slash_offsets, slash_count):
@@ -326,20 +343,21 @@
     mine = lax.all_to_all(sent, "lo", 0, 0, tiled=True)
     spread, swap, kv_own = call(
         pick_kernel,
-        (shape(2 * BLOCK, lead=NK), shape(QNAT - QDYN), shape(ROWS)),
+        (shape(2 * BLOCK, lead=NK), in_vmem(QNAT - QDYN), in_vmem(ROWS)),
         [SMEM, SMEM, VMEM],
         name="pick",
     )(meta, vertical_blocks, mine)
     row = lax.all_to_all(spread, "k", 0, 0, tiled=True).reshape(1, NK * 2 * BLOCK, DH)
+    before = lax.ppermute(kv_own, ("y", "k"), [(i, i + 1) for i in range(HI - 1)])
+    row, before = lax.optimization_barrier((row, before))
     spread_row = jnp.broadcast_to(row, (NY, NK * 2 * BLOCK, DH))
     verticals = lax.all_to_all(spread_row, "y", 0, 0, tiled=True).reshape(HI, 2 * BLOCK, DH)
     partner = [(i, i ^ 1) for i in range(LO)]
     swapped = lax.ppermute(swap, "lo", partner)
-    before = lax.ppermute(kv_own, ("y", "k"), [(i, i + 1) for i in range(HI - 1)])
     before_swap = lax.ppermute(before, "lo", partner)
-    slash, slash_stats = call(
+    slash, slash_stats, vertical_queries = call(
         slash_kernel,
-        (shape(2 * ROWS), shape(ROWS, f32)),
+        (shape(2 * ROWS), shape(ROWS, f32), shape(LO * ROWS, lead=GROUP)),
         [SMEM, VMEM, VMEM, VMEM, VMEM],
         [pltpu.VMEM((2 * LO * ROWS, DH), bf16)] * 2,
         name="slash",
@@ -347,15 +365,14 @@
     partial = call(
         vertical_kernel,
         shape(OUT_ROWS),
-        [SMEM, SMEM, VMEM, VMEM, VMEM, VMEM, VMEM],
+        [SMEM, SMEM, LOADED, VMEM, LOADED, LOADED],
         [
-            pltpu.VMEM((GROUP, LO * ROWS, DH), bf16),
             pltpu.VMEM(((NV + 1) * BLOCK, DH), bf16),
             pltpu.VMEM(((NV + 1) * BLOCK, DH), bf16),
             pltpu.VMEM((LO * ROWS, DH), f32),
         ],
         name="vertical",
-    )(meta, vertical_blocks, mine, swapped, verticals, slash, slash_stats)
+    )(meta, vertical_blocks, vertical_queries, verticals, slash, slash_stats)
     back = lax.all_to_all(partial, "lo", 0, 0, tiled=True)
     return call(
         exit_kernel,

time: 131 us -> 119 us (0.908)
  the two profiles are of different devices: /device:TPU:40 before, /device:TPU:1 now
where the time goes in v3:
time: 119 us
  starting transfers between devices  38.9 us (33%)
  waiting for transfers between devices  32 us (27%)
  Pallas kernels  21.5 us (18%)
  blocking collectives  20.4 us (17%)
  local copies, waits for them, and re-layouts  4.08 us (3%)
  other arithmetic  1.87 us (2%)
    pallas_call x5, Pallas kernels, placed(): run(*(pltpu.with_memory_space_constraint(arg, pltpu.VMEM) if spec is VMEM...  21.5 us
    all_to_all x1, blocking collectives, body(): back = lax.all_to_all(partial, 'lo', 0, 0, tiled=True)  20.4 us
    all_to_all x1, waiting for transfers between devices, body(): lax.all_to_all(spread_row, 'y', 0, 0, tiled=True).reshape(HI, 2 * BLOCK, DH)  13.9 us
    all_to_all x1, waiting for transfers between devices, body(): mine = lax.all_to_all(sent, 'lo', 0, 0, tiled=True)  13.7 us
    all_to_all x1, starting transfers between devices, body(): lax.all_to_all(spread_row, 'y', 0, 0, tiled=True).reshape(HI, 2 * BLOCK, DH)  11.5 us
    all_to_all x1, starting transfers between devices, body(): mine = lax.all_to_all(sent, 'lo', 0, 0, tiled=True)  10.3 us
    all_to_all x1, starting transfers between devices, body(): lax.all_to_all(spread, 'k', 0, 0, tiled=True).reshape(1, NK * 2 * BLOCK, DH)  6.38 us
    ppermute x1, starting transfers between devices, body(): swapped = lax.ppermute(swap, 'lo', partner)  4.62 us
  transfers between devices with their start and end apart: 6, of which 5 were waited for; matrix products, arithmetic and copies ran while one was open for 1% of the time, Pallas kernels for 5%

profile of v3, /device:TPU:1, one launch (start us, length us, event | category | flops | bytes accessed | tf_op | source)
XLA Modules:
  0.0 118.8 jit_solution(12030083084391475221)
XLA Ops:
  0.0 0.7 iota_add_fusion
  0.7 0.7 select_reduce_fusion.2
  1.7 0.9 copy.11
  2.7 0.7 copy-done.2
  3.5 0.7 concatenate.3.meta
  4.2 1.8 %entry.1 = bf16[16,224,128]{2,1,0:T(8,128)(2,1)} custom-call(s32[106]{0:T(128)} %concatenate.3.meta, bf16[32,4096]{1,0:T(8,128)(2,1)S(1)} %copy-done, bf16[32,2048]{1,0:T(8,128)(2,1)S(1)} %bitcast.8), custom_call_target="tpu_custom_call" | custom-call | tf_op jit(solution)/shard_map/entry/pallas_call | solution.py:319
  6.0 10.3 %all-to-all-start = ((bf16[16,224,128]{2,1,0:T(8,128)(2,1)}), bf16[16,224,128]{2,1,0:T(8,128)(2,1)S(1)}, u32[]{:S(2)}, u32[]{:S(2)}) async-start(bf16[16,224,128]{2,1,0:T(8,128)(2,1)} %entry.1), calls=%async_computation | async-start | bytes 1835008 | tf_op jit(solution)/shard_map/all_to_all | solution.py:343
  16.2 0.7 copy.10.vert_ref
  16.9 13.7 %all-to-all-done.in_ref = bf16[16,224,128]{2,1,0:T(8,128)(2,1)S(1)} async-done(((bf16[16,224,128]{2,1,0:T(8,128)(2,1)}), bf16[16,224,128]{2,1,0:T(8,128)(2,1)S(1)}, u32[]{:S(2)}, u32[]{:S(2)}) %all-to-all-start) | async-done | bytes 917536 | tf_op jit(solution)/shard_map/all_to_all | solution.py:343
  30.6 1.7 %pick.1 = (bf16[4,128,128]{2,1,0:T(8,128)(2,1)}, bf16[16,96,128]{2,1,0:T(8,128)(2,1)S(1)}, bf16[16,32,128]{2,1,0:T(8,128)(2,1)S(1)}) custom-call(s32[106]{0:T(128)} %concatenate.3.meta, s32[32,16]{1,0:T(8,128)} %copy.10.vert_ref, bf16[16,224,128]{2,1,0:T(8,128)(2,1)S(1)} %all-to-all-done.in_ref), custom_call_target="tpu_custom_call" | custom-call | tf_op jit(solution)/shard_map/pick/pallas_call | solution.py:319
  32.3 6.4 %all-to-all-start.1 = ((bf16[4,128,128]{2,1,0:T(8,128)(2,1)}), bf16[4,128,128]{2,1,0:T(8,128)(2,1)S(1)}, u32[]{:S(2)}, u32[]{:S(2)}) async-start(bf16[4,128,128]{2,1,0:T(8,128)(2,1)} %get-tuple-element.14), calls=%async_computation.1 | async-start | bytes 262144 | tf_op jit(solution)/shard_map/all_to_all | solution.py:350
  38.7 4.3 %collective-permute-start.1 = (bf16[16,32,128]{2,1,0:T(8,128)(2,1)S(1)}, bf16[16,32,128]{2,1,0:T(8,128)(2,1)S(1)}, u32[]{:S(2)}, u32[]{:S(2)}) collective-permute-start(bf16[16,32,128]{2,1,0:T(8,128)(2,1)S(1)} %get-tuple-element.15), channel_id=1, source_target_pairs={{0,16},{16,32},{32,48},{48,64},{64,80},{80,96},{96,112},{112,128},... | collective-permute-start | bytes 393224 | tf_op jit(solution)/shard_map/ppermute | solution.py:351
  43.0 2.4 %collective-permute-done.1.before_ref = bf16[16,32,128]{2,1,0:T(8,128)(2,1)S(1)} collective-permute-done((bf16[16,32,128]{2,1,0:T(8,128)(2,1)S(1)}, bf16[16,32,128]{2,1,0:T(8,128)(2,1)S(1)}, u32[]{:S(2)}, u32[]{:S(2)}) %collective-permute-start.1) | collective-permute-done | bytes 131104 | tf_op jit(solution)/shard_map/ppermute | solution.py:351
  45.4 0.6 all-to-all-done.1
  46.0 1.1 broadcast_in_dim.52
  47.1 11.5 %all-to-all-start.2 = ((bf16[8,512,128]{2,1,0:T(8,128)(2,1)}), bf16[8,512,128]{2,1,0:T(8,128)(2,1)S(1)}, u32[]{:S(2)}, u32[]{:S(2)}) async-start(bf16[8,512,128]{2,1,0:T(8,128)(2,1)} %broadcast_in_dim.52), calls=%async_computation.2 | async-start | bytes 2097152 | tf_op jit(solution)/shard_map/all_to_all | solution.py:354
  58.6 4.6 %collective-permute-start = (bf16[16,96,128]{2,1,0:T(8,128)(2,1)S(1)}, bf16[16,96,128]{2,1,0:T(8,128)(2,1)S(1)}, u32[]{:S(2)}, u32[]{:S(2)}) collective-permute-start(bf16[16,96,128]{2,1,0:T(8,128)(2,1)S(1)} %get-tuple-element.13), channel_id=1, source_target_pairs={{0,1},{1,0},{2,3},{3,2},{4,5},{5,4},{6,7},{7,6},{8,9},{9,8},{10,11... | collective-permute-start | bytes 1179656 | tf_op jit(solution)/shard_map/ppermute | solution.py:356
  63.2 1.9 %collective-permute-start.2 = (bf16[16,32,128]{2,1,0:T(8,128)(2,1)S(1)}, bf16[16,32,128]{2,1,0:T(8,128)(2,1)S(1)}, u32[]{:S(2)}, u32[]{:S(2)}) collective-permute-start(bf16[16,32,128]{2,1,0:T(8,128)(2,1)S(1)} %collective-permute-done.1.before_ref), channel_id=1, source_target_pairs={{0,1},{1,0},{2,3},{3,2},{4,5},{5,4},{6,7},{7,6},{8,9},{9,8},{10,11... | collective-permute-start | bytes 393224 | tf_op jit(solution)/shard_map/ppermute | solution.py:357
  65.2 1.3 %collective-permute-done.2.before_swap_ref = bf16[16,32,128]{2,1,0:T(8,128)(2,1)S(1)} collective-permute-done((bf16[16,32,128]{2,1,0:T(8,128)(2,1)S(1)}, bf16[16,32,128]{2,1,0:T(8,128)(2,1)S(1)}, u32[]{:S(2)}, u32[]{:S(2)}) %collective-permute-start.2) | collective-permute-done | bytes 131104 | tf_op jit(solution)/shard_map/ppermute | solution.py:357
  66.5 5.4 %slash.1 = (bf16[16,64,128]{2,1,0:T(8,128)(2,1)}, f32[16,32,128]{2,1,0:T(8,128)}, bf16[4,512,128]{2,1,0:T(8,128)(2,1)}) custom-call(s32[106]{0:T(128)} %concatenate.3.meta, bf16[16,224,128]{2,1,0:T(8,128)(2,1)S(1)} %all-to-all-done.in_ref, bf16[16,96,128]{2,1,0:T(8,128)(2,1)S(1)} %collective-permute-done.swap_ref, ...), custom_call_target="tpu_custom_call" | custom-call | tf_op jit(solution)/shard_map/slash/pallas_call | solution.py:319
  71.9 13.9 %all-to-all-done.2 = bf16[8,512,128]{2,1,0:T(8,128)(2,1)S(1)} async-done(((bf16[8,512,128]{2,1,0:T(8,128)(2,1)}), bf16[8,512,128]{2,1,0:T(8,128)(2,1)S(1)}, u32[]{:S(2)}, u32[]{:S(2)}) %all-to-all-start.2) | async-done | bytes 1048608 | tf_op jit(solution)/shard_map/all_to_all | solution.py:354
  85.9 9.9 %vertical.1 = bf16[16,224,128]{2,1,0:T(8,128)(2,1)} custom-call(s32[106]{0:T(128)} %concatenate.3.meta, s32[32,16]{1,0:T(8,128)} %copy.10.vert_ref, bf16[4,512,128]{2,1,0:T(8,128)(2,1)} %get-tuple-element.17.q_buf, bf16[32,128,128]{2,1,0:T(8,128)(2,1)S(1)} %bitcast.7, bf16[16,64,128]{2,1,0:T(8,128)(2,1)} %get-tuple-element.19.slash_ref, ...), custom_call_target="tpu_custom_call" | custom-call | tf_op jit(solution)/shard_map/vertical/pallas_call | solution.py:319
  95.7 20.4 %all_to_all.20.in_ref = bf16[16,224,128]{2,1,0:T(8,128)(2,1)S(1)} all-to-all(bf16[16,224,128]{2,1,0:T(8,128)(2,1)} %vertical.1), channel_id=1, replica_groups=mesh['y'=8,'k'=4,'lo'=16] {'lo'}, dimensions={0} | all-to-all | bytes 1835008 | tf_op jit(solution)/shard_map/all_to_all | solution.py:376
  116.1 2.7 %exit.1 = bf16[32,4096]{1,0:T(8,128)(2,1)} custom-call(s32[106]{0:T(128)} %concatenate.3.meta, bf16[16,224,128]{2,1,0:T(8,128)(2,1)S(1)} %all_to_all.20.in_ref, bf16[32,4096]{1,0:T(8,128)(2,1)S(1)} %copy-done.1), custom_call_target="tpu_custom_call" | custom-call | tf_op jit(solution)/shard_map/exit/pallas_call | solution.py:319
  (11 shorter events, 0.5 us)
Async XLA Ops:
  0.0 4.2 %copy-start = (bf16[32,4096]{1,0:T(8,128)(2,1)S(1)}, bf16[32,4096]{1,0:T(8,128)(2,1)}, u32[]{:S(2)}) copy-start(bf16[32,4096]{1,0:T(8,128)(2,1)} %q_ref.1) | copy-start | bytes 786436
  2.7 0.7 copy-start.2
  6.0 24.6 %all-to-all-start = ((bf16[16,224,128]{2,1,0:T(8,128)(2,1)}), bf16[16,224,128]{2,1,0:T(8,128)(2,1)S(1)}, u32[]{:S(2)}, u32[]{:S(2)}) async-start(bf16[16,224,128]{2,1,0:T(8,128)(2,1)} %entry.1), calls=%async_computation | async-start | bytes 1835008 | tf_op jit(solution)/shard_map/all_to_all | solution.py:343
  32.3 13.7 %all-to-all-start.1 = ((bf16[4,128,128]{2,1,0:T(8,128)(2,1)}), bf16[4,128,128]{2,1,0:T(8,128)(2,1)S(1)}, u32[]{:S(2)}, u32[]{:S(2)}) async-start(bf16[4,128,128]{2,1,0:T(8,128)(2,1)} %get-tuple-element.14), calls=%async_computation.1 | async-start | bytes 262144 | tf_op jit(solution)/shard_map/all_to_all | solution.py:350
  38.7 6.7 %collective-permute-start.1 = (bf16[16,32,128]{2,1,0:T(8,128)(2,1)S(1)}, bf16[16,32,128]{2,1,0:T(8,128)(2,1)S(1)}, u32[]{:S(2)}, u32[]{:S(2)}) collective-permute-start(bf16[16,32,128]{2,1,0:T(8,128)(2,1)S(1)} %get-tuple-element.15), channel_id=1, source_target_pairs={{0,16},{16,32},{32,48},{48,64},{64,80},{80,96},{96,112},{112,128},... | collective-permute-start | bytes 393224 | tf_op jit(solution)/shard_map/ppermute | solution.py:351
  47.1 38.7 %all-to-all-start.2 = ((bf16[8,512,128]{2,1,0:T(8,128)(2,1)}), bf16[8,512,128]{2,1,0:T(8,128)(2,1)S(1)}, u32[]{:S(2)}, u32[]{:S(2)}) async-start(bf16[8,512,128]{2,1,0:T(8,128)(2,1)} %broadcast_in_dim.52), calls=%async_computation.2 | async-start | bytes 2097152 | tf_op jit(solution)/shard_map/all_to_all | solution.py:354
  58.6 7.9 %collective-permute-start = (bf16[16,96,128]{2,1,0:T(8,128)(2,1)S(1)}, bf16[16,96,128]{2,1,0:T(8,128)(2,1)S(1)}, u32[]{:S(2)}, u32[]{:S(2)}) collective-permute-start(bf16[16,96,128]{2,1,0:T(8,128)(2,1)S(1)} %get-tuple-element.13), channel_id=1, source_target_pairs={{0,1},{1,0},{2,3},{3,2},{4,5},{5,4},{6,7},{7,6},{8,9},{9,8},{10,11... | collective-permute-start | bytes 1179656 | tf_op jit(solution)/shard_map/ppermute | solution.py:356
  63.2 3.2 %collective-permute-start.2 = (bf16[16,32,128]{2,1,0:T(8,128)(2,1)S(1)}, bf16[16,32,128]{2,1,0:T(8,128)(2,1)S(1)}, u32[]{:S(2)}, u32[]{:S(2)}) collective-permute-start(bf16[16,32,128]{2,1,0:T(8,128)(2,1)S(1)} %collective-permute-done.1.before_ref), channel_id=1, source_target_pairs={{0,1},{1,0},{2,3},{3,2},{4,5},{5,4},{6,7},{7,6},{8,9},{9,8},{10,11... | collective-permute-start | bytes 393224 | tf_op jit(solution)/shard_map/ppermute | solution.py:357
  95.7 20.4 %copy-start.1 = (bf16[32,4096]{1,0:T(8,128)(2,1)S(1)}, bf16[32,4096]{1,0:T(8,128)(2,1)}, u32[]{:S(2)}) copy-start(bf16[32,4096]{1,0:T(8,128)(2,1)} %gate_ref.1) | copy-start | bytes 786436

commit v4 on v3

--- a/solution.py
+++ b/solution.py
@@ -19,6 +19,7 @@
 HI = NY * NK
 GROUP = 4
 LOWEST = -3.0e38
+STEPS = 2
 EXP2_SCALE = DH**-0.5 * 1.4426950408889634
 
 VERT, QDYN, KVNAT, QNAT, IN_ROWS = 0, 64, 128, 160, 224
@@ -26,7 +27,8 @@
 SLOTS = GROUP + 2
 L_LANE = 8
 PART = 32
-M_HEAD, M_SLOT, M_MASK, M_KV, M_HI, M_LO, M_LEN = 0, 32, 64, 96, 104, 105, 106
+M_HEAD, M_SLOT, M_MASK, M_HI, M_LO = 0, 32, 64, 96, 97
+E_HEAD, E_KV = 0, 32
 
 bf16 = jnp.bfloat16
 f32 = jnp.float32
@@ -59,7 +61,8 @@
         ),
         axis=1,
     )
-    return jnp.concatenate([head_of, slot, mask, kv_of, jnp.stack([hi, lo])]).astype(jnp.int32)
+    entry = jnp.concatenate([head_of, kv_of]).astype(jnp.int32)
+    return entry, jnp.concatenate([head_of, slot, mask, jnp.stack([hi, lo])]).astype(jnp.int32)
 
 
 def entry_kernel(meta, q_ref, kv_ref, out_ref):
@@ -70,10 +73,10 @@
         return kv_ref[:, pl.ds(pl.multiple_of(which * KVH * DH + head * DH, DH), DH)]
 
     for g in range(KVH):
-        kv_head = meta[M_KV + g]
+        kv_head = meta[E_KV + g]
         vert = [kv_cols(0, kv_head), kv_cols(1, kv_head)]
         for c in range(2):
-            parts = vert + [q_cols(meta[M_HEAD + g * GROUP + 2 * c + p]) for p in range(2)]
+            parts = vert + [q_cols(meta[E_HEAD + g * GROUP + 2 * c + p]) for p in range(2)]
             parts += [kv_cols(c, g), q_cols(4 * g + 2 * c), q_cols(4 * g + 2 * c + 1)]
             for n, part in enumerate(parts):
                 out_ref[2 * g + c, n * ROWS : (n + 1) * ROWS, :] = part
@@ -95,7 +98,7 @@
         for which in range(2):
             part = in_ref[first + half, VERT + which * ROWS : VERT + (which + 1) * ROWS, :]
             at = which * BLOCK + half * ROWS
-            for d in range(NK):
+            for d in range(HI):
                 spread_ref[d, at : at + ROWS, :] = part
     swap_ref[...] = in_ref[:, QDYN:QNAT, :]
     kv_ref[...] = in_ref[:, KVNAT:QNAT, :]
@@ -202,7 +205,6 @@
     k_buf[...] = jnp.zeros(k_buf.shape, bf16)
     v_buf[...] = jnp.zeros(v_buf.shape, bf16)
     of_lane = lax.broadcasted_iota(jnp.int32, (1, width), 1) // BLOCK
-    lane = lax.broadcasted_iota(jnp.int32, (2 * BLOCK, DH), 1)
 
     def head_step(p, _):
         head = meta[M_HEAD + g * GROUP + p]
@@ -222,12 +224,14 @@
         def attend(n):
             size = n * BLOCK
 
-            def step(i, _):
-                at = pl.multiple_of(i * 2 * BLOCK, 2 * BLOCK)
-                s = scores(q_buf[p, pl.ds(at, 2 * BLOCK), :], k_buf[0:size, :])
+            rows = LO * ROWS // STEPS
+            lane = lax.broadcasted_iota(jnp.int32, (rows, DH), 1)
+            for i in range(STEPS):
+                span = slice(i * rows, (i + 1) * rows)
+                s = scores(q_buf[p, span, :], k_buf[0:size, :])
                 parts = []
-                for t in range(2):
-                    distance = first_block + 2 * i + t - ids[:, 0:size]
+                for t in range(rows // BLOCK):
+                    distance = first_block + i * (rows // BLOCK) + t - ids[:, 0:size]
                     slashed = jnp.right_shift(mask[:, 0:size], jnp.clip(distance, 0, 31)) & 1
                     bias = jnp.where((distance > 0) & (slashed == 0), 0.0, -jnp.inf)
                     parts.append(s[t * BLOCK : (t + 1) * BLOCK] + bias)
@@ -236,14 +240,12 @@
                 e = jnp.exp2((s - top) * EXP2_SCALE)
                 total = jnp.sum(e, axis=1, keepdims=True)
                 acc = jnp.dot(e.astype(bf16), v_buf[0:size, :], preferred_element_type=f32)
-                rows = pl.ds(pl.multiple_of(OV + p * ROWS, ROWS), ROWS)
-                out_ref[pl.ds(4 * i, 4), rows, :] = acc.astype(bf16).reshape(4, ROWS, DH)
-                tile = stats_buf[pl.ds(at, 2 * BLOCK), :]
-                tile = jnp.where(lane == p, top, tile)
-                stats_buf[pl.ds(at, 2 * BLOCK), :] = jnp.where(lane == L_LANE + p, total, tile)
-                return 0
-
-            lax.fori_loop(0, 4, step, 0)
+                held = slice(i * rows // ROWS, (i + 1) * rows // ROWS)
+                out_ref[held, pl.ds(pl.multiple_of(OV + p * ROWS, ROWS), ROWS), :] = acc.astype(
+                    bf16
+                ).reshape(rows // ROWS, ROWS, DH)
+                tile = jnp.where(lane == p, top, stats_buf[span, :])
+                stats_buf[span, :] = jnp.where(lane == L_LANE + p, total, tile)
 
         for low, n in ((-1, 8), (8, 12), (12, 16)):
 
@@ -304,14 +306,13 @@
     lax.fori_loop(0, LO, source_step, 0, unroll=2)
 
 
-def call(kernel, out_shape, in_specs, scratch=(), name=None, **options):
+def call(kernel, out_shape, in_specs, scratch=(), **options):
     run = pl.pallas_call(
         kernel,
         out_shape=out_shape,
         in_specs=in_specs,
         out_specs=tuple(VMEM for _ in out_shape) if isinstance(out_shape, tuple) else VMEM,
         scratch_shapes=list(scratch),
-        name=name,
         **options,
     )
 
@@ -335,23 +336,17 @@
 
 
 def body(queries, key_values, gate_logits, vertical_blocks, slash_offsets, slash_count):
-    meta = tables(vertical_blocks, slash_offsets, slash_count)
+    entry_meta, meta = tables(vertical_blocks, slash_offsets, slash_count)
     flat_kv = key_values.reshape(ROWS, 2 * KVH * DH)
-    sent = call(entry_kernel, shape(IN_ROWS), [SMEM, VMEM, VMEM], name="entry")(
-        meta, queries, flat_kv
-    )
+    sent = call(entry_kernel, shape(IN_ROWS), [SMEM, VMEM, VMEM])(entry_meta, queries, flat_kv)
     mine = lax.all_to_all(sent, "lo", 0, 0, tiled=True)
     spread, swap, kv_own = call(
         pick_kernel,
-        (shape(2 * BLOCK, lead=NK), in_vmem(QNAT - QDYN), in_vmem(ROWS)),
+        (shape(2 * BLOCK, lead=HI), in_vmem(QNAT - QDYN), in_vmem(ROWS)),
         [SMEM, SMEM, VMEM],
-        name="pick",
     )(meta, vertical_blocks, mine)
-    row = lax.all_to_all(spread, "k", 0, 0, tiled=True).reshape(1, NK * 2 * BLOCK, DH)
     before = lax.ppermute(kv_own, ("y", "k"), [(i, i + 1) for i in range(HI - 1)])
-    row, before = lax.optimization_barrier((row, before))
-    spread_row = jnp.broadcast_to(row, (NY, NK * 2 * BLOCK, DH))
-    verticals = lax.all_to_all(spread_row, "y", 0, 0, tiled=True).reshape(HI, 2 * BLOCK, DH)
+    verticals = lax.all_to_all(spread, ("y", "k"), 0, 0, tiled=True)
     partner = [(i, i ^ 1) for i in range(LO)]
     swapped = lax.ppermute(swap, "lo", partner)
     before_swap = lax.ppermute(before, "lo", partner)
@@ -360,7 +355,6 @@
         (shape(2 * ROWS), shape(ROWS, f32), shape(LO * ROWS, lead=GROUP)),
         [SMEM, VMEM, VMEM, VMEM, VMEM],
         [pltpu.VMEM((2 * LO * ROWS, DH), bf16)] * 2,
-        name="slash",
     )(meta, mine, swapped, before, before_swap)
     partial = call(
         vertical_kernel,
@@ -371,7 +365,6 @@
             pltpu.VMEM(((NV + 1) * BLOCK, DH), bf16),
             pltpu.VMEM((LO * ROWS, DH), f32),
         ],
-        name="vertical",
     )(meta, vertical_blocks, vertical_queries, verticals, slash, slash_stats)
     back = lax.all_to_all(partial, "lo", 0, 0, tiled=True)
     return call(
@@ -379,13 +372,13 @@
         jax.ShapeDtypeStruct((ROWS, H * DH), bf16),
         [SMEM, VMEM, VMEM],
         [pltpu.VMEM((LO, ROWS, SLOTS * DH), f32)] * 2,
-        name="exit",
     )(meta, back, gate_logits)
 
 
 def solution(mesh):
     pairs = Mesh(mesh.devices.reshape(NY, NK, LO), ("y", "k", "lo"))
     tokens = P(("y", "k", "lo"))
+
     return jax.shard_map(
         body,
         mesh=pairs,

time: 119 us -> 115 us (0.966)
  the two profiles are of different devices: /device:TPU:1 before, /device:TPU:24 now
where the time goes in v4:
time: 115 us; the launch traced here: 114 us
  waiting for transfers between devices  42.5 us (37%)
  starting transfers between devices  29.4 us (26%)
  blocking collectives  18.8 us (16%)
  Pallas kernels  18.4 us (16%)
  local copies, waits for them, and re-layouts  2.97 us (3%)
  other arithmetic  1.83 us (2%)
    ppermute x1, waiting for transfers between devices, body(): lax.ppermute(kv_own, ('y', 'k'), [(i, i + 1) for i in range(HI - 1)])  27.4 us
    all_to_all x1, blocking collectives, body(): back = lax.all_to_all(partial, 'lo', 0, 0, tiled=True)  18.8 us
    pallas_call x5, Pallas kernels, placed(): run(*(pltpu.with_memory_space_constraint(arg, pltpu.VMEM) if spec is VMEM...  18.4 us
    all_to_all x1, starting transfers between devices, body(): verticals = lax.all_to_all(spread, ('y', 'k'), 0, 0, tiled=True)  15.1 us
    all_to_all x1, waiting for transfers between devices, body(): mine = lax.all_to_all(sent, 'lo', 0, 0, tiled=True)  13.7 us
    all_to_all x1, starting transfers between devices, body(): mine = lax.all_to_all(sent, 'lo', 0, 0, tiled=True)  6.21 us
    ppermute x1, starting transfers between devices, body(): lax.ppermute(kv_own, ('y', 'k'), [(i, i + 1) for i in range(HI - 1)])  4.27 us
  transfers between devices with their start and end apart: 5, of which 3 were waited for; matrix products, arithmetic and copies ran while one was open for 1% of the time, Pallas kernels for 5%

profile of v4, /device:TPU:24, one launch (start us, length us, event | category | flops | bytes accessed | tf_op | source)
XLA Modules:
  0.0 113.9 jit_solution(5882607731052066560)
XLA Ops:
  0.0 0.7 iota_add_fusion
  0.7 0.2 convert_reduce_fusion
  0.9 0.1 select_reduce_fusion
  1.0 0.9 copy.11
  2.0 0.0 copy-start.2
  2.0 0.7 copy-done.2
  2.7 0.1 select_reduce_fusion.1
  2.8 0.7 pad_add_fusion.meta
  3.5 1.8 %shard_map.64 = bf16[16,224,128]{2,1,0:T(8,128)(2,1)} custom-call(s32[40]{0:T(128)} %pad_add_fusion.meta, bf16[32,4096]{1,0:T(8,128)(2,1)S(1)} %copy-done, bf16[32,2048]{1,0:T(8,128)(2,1)S(1)} %bitcast.4), custom_call_target="tpu_custom_call" | custom-call | tf_op jit(solution)/shard_map/pallas_call | solution.py:320
  5.2 6.2 %all-to-all-start = ((bf16[16,224,128]{2,1,0:T(8,128)(2,1)}), bf16[16,224,128]{2,1,0:T(8,128)(2,1)S(1)}, u32[]{:S(2)}, u32[]{:S(2)}) async-start(bf16[16,224,128]{2,1,0:T(8,128)(2,1)} %shard_map.64), calls=%async_computation | async-start | bytes 1835008 | tf_op jit(solution)/shard_map/all_to_all | solution.py:342
  11.5 0.7 copy.10.vert_ref
  12.2 0.7 concatenate.6.meta
  12.9 13.7 %all-to-all-done.in_ref = bf16[16,224,128]{2,1,0:T(8,128)(2,1)S(1)} async-done(((bf16[16,224,128]{2,1,0:T(8,128)(2,1)}), bf16[16,224,128]{2,1,0:T(8,128)(2,1)S(1)}, u32[]{:S(2)}, u32[]{:S(2)}) %all-to-all-start) | async-done | bytes 917536 | tf_op jit(solution)/shard_map/all_to_all | solution.py:342
  26.6 2.3 %shard_map.65 = (bf16[32,128,128]{2,1,0:T(8,128)(2,1)}, bf16[16,96,128]{2,1,0:T(8,128)(2,1)S(1)}, bf16[16,32,128]{2,1,0:T(8,128)(2,1)S(1)}) custom-call(s32[98]{0:T(128)} %concatenate.6.meta, s32[32,16]{1,0:T(8,128)} %copy.10.vert_ref, bf16[16,224,128]{2,1,0:T(8,128)(2,1)S(1)} %all-to-all-done.in_ref), custom_call_target="tpu_custom_call" | custom-call | tf_op jit(solution)/shard_map/pallas_call | solution.py:320
  28.9 15.1 %all-to-all-start.1 = ((bf16[32,128,128]{2,1,0:T(8,128)(2,1)}), bf16[32,128,128]{2,1,0:T(8,128)(2,1)S(1)}, u32[]{:S(2)}, u32[]{:S(2)}) async-start(bf16[32,128,128]{2,1,0:T(8,128)(2,1)} %get-tuple-element.14), calls=%async_computation.1 | async-start | bytes 2097152 | tf_op jit(solution)/shard_map/all_to_all | solution.py:349
  43.9 1.9 %collective-permute-start = (bf16[16,96,128]{2,1,0:T(8,128)(2,1)S(1)}, bf16[16,96,128]{2,1,0:T(8,128)(2,1)S(1)}, u32[]{:S(2)}, u32[]{:S(2)}) collective-permute-start(bf16[16,96,128]{2,1,0:T(8,128)(2,1)S(1)} %get-tuple-element.11), channel_id=1, source_target_pairs={{0,1},{1,0},{2,3},{3,2},{4,5},{5,4},{6,7},{7,6},{8,9},{9,8},{10,11... | collective-permute-start | bytes 1179656 | tf_op jit(solution)/shard_map/ppermute | solution.py:351
  45.8 4.3 %collective-permute-start.1 = (bf16[16,32,128]{2,1,0:T(8,128)(2,1)S(1)}, bf16[16,32,128]{2,1,0:T(8,128)(2,1)S(1)}, u32[]{:S(2)}, u32[]{:S(2)}) collective-permute-start(bf16[16,32,128]{2,1,0:T(8,128)(2,1)S(1)} %get-tuple-element.12), channel_id=1, source_target_pairs={{0,16},{16,32},{32,48},{48,64},{64,80},{80,96},{96,112},{112,128},... | collective-permute-start | bytes 393224 | tf_op jit(solution)/shard_map/ppermute | solution.py:348
  50.1 27.4 %collective-permute-done.1.before_ref = bf16[16,32,128]{2,1,0:T(8,128)(2,1)S(1)} collective-permute-done((bf16[16,32,128]{2,1,0:T(8,128)(2,1)S(1)}, bf16[16,32,128]{2,1,0:T(8,128)(2,1)S(1)}, u32[]{:S(2)}, u32[]{:S(2)}) %collective-permute-start.1) | collective-permute-done | bytes 131104 | tf_op jit(solution)/shard_map/ppermute | solution.py:348
  77.5 1.9 %collective-permute-start.2 = (bf16[16,32,128]{2,1,0:T(8,128)(2,1)S(1)}, bf16[16,32,128]{2,1,0:T(8,128)(2,1)S(1)}, u32[]{:S(2)}, u32[]{:S(2)}) collective-permute-start(bf16[16,32,128]{2,1,0:T(8,128)(2,1)S(1)} %collective-permute-done.1.before_ref), channel_id=1, source_target_pairs={{0,1},{1,0},{2,3},{3,2},{4,5},{5,4},{6,7},{7,6},{8,9},{9,8},{10,11... | collective-permute-start | bytes 393224 | tf_op jit(solution)/shard_map/ppermute | solution.py:352
  79.5 1.3 %collective-permute-done.2.before_swap_ref = bf16[16,32,128]{2,1,0:T(8,128)(2,1)S(1)} collective-permute-done((bf16[16,32,128]{2,1,0:T(8,128)(2,1)S(1)}, bf16[16,32,128]{2,1,0:T(8,128)(2,1)S(1)}, u32[]{:S(2)}, u32[]{:S(2)}) %collective-permute-start.2) | collective-permute-done | bytes 131104 | tf_op jit(solution)/shard_map/ppermute | solution.py:352
  80.8 5.4 %shard_map.66 = (bf16[16,64,128]{2,1,0:T(8,128)(2,1)}, f32[16,32,128]{2,1,0:T(8,128)}, bf16[4,512,128]{2,1,0:T(8,128)(2,1)}) custom-call(s32[98]{0:T(128)} %concatenate.6.meta, bf16[16,224,128]{2,1,0:T(8,128)(2,1)S(1)} %all-to-all-done.in_ref, bf16[16,96,128]{2,1,0:T(8,128)(2,1)S(1)} %collective-permute-done.swap_ref, ...), custom_call_target="tpu_custom_call" | custom-call | tf_op jit(solution)/shard_map/pallas_call | solution.py:320
  86.2 6.2 %shard_map.67 = bf16[16,224,128]{2,1,0:T(8,128)(2,1)} custom-call(s32[98]{0:T(128)} %concatenate.6.meta, s32[32,16]{1,0:T(8,128)} %copy.10.vert_ref, bf16[4,512,128]{2,1,0:T(8,128)(2,1)} %get-tuple-element.13.q_buf, bf16[32,128,128]{2,1,0:T(8,128)(2,1)S(1)} %all-to-all-done.1.all_ref, bf16[16,64,128]{2,1,0:T(8,128)(2,1)} %get-tuple-element.15.slash_ref, ...), custom_call_target="tpu_custom_call" | custom-call | tf_op jit(solution)/shard_map/pallas_call | solution.py:320
  92.4 18.8 %all_to_all.15.in_ref = bf16[16,224,128]{2,1,0:T(8,128)(2,1)S(1)} all-to-all(bf16[16,224,128]{2,1,0:T(8,128)(2,1)} %shard_map.67), channel_id=1, replica_groups=mesh['y'=8,'k'=4,'lo'=16] {'lo'}, dimensions={0} | all-to-all | bytes 1835008 | tf_op jit(solution)/shard_map/all_to_all | solution.py:369
  111.2 2.7 %shard_map.68 = bf16[32,4096]{1,0:T(8,128)(2,1)} custom-call(s32[98]{0:T(128)} %concatenate.6.meta, bf16[16,224,128]{2,1,0:T(8,128)(2,1)S(1)} %all_to_all.15.in_ref, bf16[32,4096]{1,0:T(8,128)(2,1)S(1)} %copy-done.1), custom_call_target="tpu_custom_call" | custom-call | tf_op jit(solution)/shard_map/pallas_call | solution.py:320
  (13 shorter events, 0.1 us)
Async XLA Ops:
  0.0 3.5 %copy-start = (bf16[32,4096]{1,0:T(8,128)(2,1)S(1)}, bf16[32,4096]{1,0:T(8,128)(2,1)}, u32[]{:S(2)}) copy-start(bf16[32,4096]{1,0:T(8,128)(2,1)} %q_ref.1) | copy-start | bytes 786436
  2.0 0.7 copy-start.2
  5.2 21.4 %all-to-all-start = ((bf16[16,224,128]{2,1,0:T(8,128)(2,1)}), bf16[16,224,128]{2,1,0:T(8,128)(2,1)S(1)}, u32[]{:S(2)}, u32[]{:S(2)}) async-start(bf16[16,224,128]{2,1,0:T(8,128)(2,1)} %shard_map.64), calls=%async_computation | async-start | bytes 1835008 | tf_op jit(solution)/shard_map/all_to_all | solution.py:342
  11.5 0.7 copy-start.3
  11.5 0.7 copy-start.4
  28.9 57.3 %all-to-all-start.1 = ((bf16[32,128,128]{2,1,0:T(8,128)(2,1)}), bf16[32,128,128]{2,1,0:T(8,128)(2,1)S(1)}, u32[]{:S(2)}, u32[]{:S(2)}) async-start(bf16[32,128,128]{2,1,0:T(8,128)(2,1)} %get-tuple-element.14), calls=%async_computation.1 | async-start | bytes 2097152 | tf_op jit(solution)/shard_map/all_to_all | solution.py:349
  43.9 36.9 %collective-permute-start = (bf16[16,96,128]{2,1,0:T(8,128)(2,1)S(1)}, bf16[16,96,128]{2,1,0:T(8,128)(2,1)S(1)}, u32[]{:S(2)}, u32[]{:S(2)}) collective-permute-start(bf16[16,96,128]{2,1,0:T(8,128)(2,1)S(1)} %get-tuple-element.11), channel_id=1, source_target_pairs={{0,1},{1,0},{2,3},{3,2},{4,5},{5,4},{6,7},{7,6},{8,9},{9,8},{10,11... | collective-permute-start | bytes 1179656 | tf_op jit(solution)/shard_map/ppermute | solution.py:351
  45.8 31.7 %collective-permute-start.1 = (bf16[16,32,128]{2,1,0:T(8,128)(2,1)S(1)}, bf16[16,32,128]{2,1,0:T(8,128)(2,1)S(1)}, u32[]{:S(2)}, u32[]{:S(2)}) collective-permute-start(bf16[16,32,128]{2,1,0:T(8,128)(2,1)S(1)} %get-tuple-element.12), channel_id=1, source_target_pairs={{0,16},{16,32},{32,48},{48,64},{64,80},{80,96},{96,112},{112,128},... | collective-permute-start | bytes 393224 | tf_op jit(solution)/shard_map/ppermute | solution.py:348
  77.5 3.2 %collective-permute-start.2 = (bf16[16,32,128]{2,1,0:T(8,128)(2,1)S(1)}, bf16[16,32,128]{2,1,0:T(8,128)(2,1)S(1)}, u32[]{:S(2)}, u32[]{:S(2)}) collective-permute-start(bf16[16,32,128]{2,1,0:T(8,128)(2,1)S(1)} %collective-permute-done.1.before_ref), channel_id=1, source_target_pairs={{0,1},{1,0},{2,3},{3,2},{4,5},{5,4},{6,7},{7,6},{8,9},{9,8},{10,11... | collective-permute-start | bytes 393224 | tf_op jit(solution)/shard_map/ppermute | solution.py:352
  92.4 18.8 %copy-start.1 = (bf16[32,4096]{1,0:T(8,128)(2,1)S(1)}, bf16[32,4096]{1,0:T(8,128)(2,1)}, u32[]{:S(2)}) copy-start(bf16[32,4096]{1,0:T(8,128)(2,1)} %gate_ref.1) | copy-start | bytes 786436

commit v5 on v4

--- a/solution.py
+++ b/solution.py
@@ -22,13 +22,14 @@
 STEPS = 2
 EXP2_SCALE = DH**-0.5 * 1.4426950408889634
 
-VERT, QDYN, KVNAT, QNAT, IN_ROWS = 0, 64, 128, 160, 224
-OV, OS, STATS, OUT_ROWS = 0, 128, 192, 224
+VERT, KVNAT, QDYN, QNAT, IN_ROWS = 0, 64, 0, 128, 192
+KV_ROWS = QNAT - KVNAT
+OV, OS, STATS, OUT_ROWS = 0, 128, 192, 208
 SLOTS = GROUP + 2
 L_LANE = 8
-PART = 32
-M_HEAD, M_SLOT, M_MASK, M_HI, M_LO = 0, 32, 64, 96, 97
-E_HEAD, E_KV = 0, 32
+PART = 16
+M_HEAD, M_SLOT, M_MASK, M_HI, M_LO, M_BLOCK = 0, 32, 64, 96, 97, 98
+E_HEAD, E_KV, E_ZL = 0, 32, 40
 
 bf16 = jnp.bfloat16
 f32 = jnp.float32
@@ -61,8 +62,11 @@
         ),
         axis=1,
     )
-    entry = jnp.concatenate([head_of, kv_of]).astype(jnp.int32)
-    return entry, jnp.concatenate([head_of, slot, mask, jnp.stack([hi, lo])]).astype(jnp.int32)
+    taken = (group == lo // 2)[:, None] & (vertical_blocks // 4 == hi * 2 + lo % 2)
+    block = jnp.sum(jnp.where(taken, vertical_blocks % 4, 0))
+    entry = jnp.concatenate([head_of, kv_of, (lo // (LO // 2))[None]]).astype(jnp.int32)
+    rest = jnp.concatenate([head_of, slot, mask, jnp.stack([hi, lo, block])])
+    return entry, rest.astype(jnp.int32)
 
 
 def entry_kernel(meta, q_ref, kv_ref, out_ref):
@@ -72,36 +76,31 @@
     def kv_cols(which, head):
         return kv_ref[:, pl.ds(pl.multiple_of(which * KVH * DH + head * DH, DH), DH)]
 
+    zl = meta[E_ZL]
     for g in range(KVH):
         kv_head = meta[E_KV + g]
-        vert = [kv_cols(0, kv_head), kv_cols(1, kv_head)]
-        for c in range(2):
-            parts = vert + [q_cols(meta[E_HEAD + g * GROUP + 2 * c + p]) for p in range(2)]
-            parts += [kv_cols(c, g), q_cols(4 * g + 2 * c), q_cols(4 * g + 2 * c + 1)]
-            for n, part in enumerate(parts):
-                out_ref[2 * g + c, n * ROWS : (n + 1) * ROWS, :] = part
-
-
-def pick_kernel(meta, vert_ref, in_ref, spread_ref, swap_ref, kv_ref):
-    lo = meta[M_LO]
-    g = lo >> 1
-    c = lo & 1
-    shard = meta[M_HI] * 2 + c
-    block = jnp.int32(0)
-    for p in range(GROUP):
-        head = meta[M_HEAD + g * GROUP + p]
-        for j in range(NV):
-            v = vert_ref[head, j]
-            block = jnp.where((v >> 2) == shard, v & 3, block)
-    first = c * (LO // 2) + 2 * block
-    for half in range(2):
+        near = [kv_cols(0, kv_head), kv_cols(1, kv_head), kv_cols(0, g), kv_cols(1, g)]
+        far = [q_cols(meta[E_HEAD + g * GROUP + p]) for p in range(GROUP)]
+        for core, parts in ((zl, near), (1 - zl, far)):
+            own = [q_cols(4 * g + 2 * core + a) for a in range(2)]
+            for n, part in enumerate(parts + own):
+                out_ref[2 * g + core, n * ROWS : (n + 1) * ROWS, :] = part
+
+
+def pick_kernel(meta, in_ref, spread_ref, swap_ref, kv_ref):
+    c = meta[M_LO] & 1
+    half = LO // 2
+    first = c * half + 2 * meta[M_BLOCK]
+    for side in range(2):
         for which in range(2):
-            part = in_ref[first + half, VERT + which * ROWS : VERT + (which + 1) * ROWS, :]
-            at = which * BLOCK + half * ROWS
+            part = in_ref[first + side, VERT + which * ROWS : VERT + (which + 1) * ROWS, :]
+            at = which * BLOCK + side * ROWS
             for d in range(HI):
                 spread_ref[d, at : at + ROWS, :] = part
-    swap_ref[...] = in_ref[:, QDYN:QNAT, :]
-    kv_ref[...] = in_ref[:, KVNAT:QNAT, :]
+    kv = in_ref[pl.ds(c * half, half), KVNAT:QNAT, :]
+    kv_ref[...] = kv
+    swap_ref[:, 0:KV_ROWS, :] = kv
+    swap_ref[:, KV_ROWS:, :] = in_ref[pl.ds((1 - c) * half, half), QDYN:QNAT, :]
 
 
 def scores(q, k):
@@ -111,22 +110,27 @@
 def slash_kernel(
     meta, in_ref, swap_ref, before_ref, before_swap_ref, out_ref, stats_ref, q_ref, k_buf, v_buf
 ):
-    half = LO * ROWS
     lo = meta[M_LO]
     core = lo & 1
-    for t in range(2):
-        rows = slice(t * ROWS, (t + 1) * ROWS)
-        q_ref[2 * core + t] = in_ref[:, QDYN + t * ROWS : QDYN + (t + 1) * ROWS, :].reshape(half, DH)
-        q_ref[2 * (1 - core) + t] = swap_ref[:, rows, :].reshape(half, DH)
-    for c in range(2):
-
-        @pl.when((lo & 1) == c)
-        def _(c=c):
-            mine, other = (k_buf, v_buf) if c == 0 else (v_buf, k_buf)
-            mine[0:half, :] = before_ref[...].reshape(half, DH)
-            other[0:half, :] = before_swap_ref[...].reshape(half, DH)
-            mine[half:, :] = in_ref[:, KVNAT:QNAT, :].reshape(half, DH)
-            other[half:, :] = swap_ref[:, KVNAT - QDYN :, :].reshape(half, DH)
+    some = LO // 2
+    shard = some * ROWS
+    pair = 2 * shard
+    mine = pl.multiple_of(core * shard, shard)
+    other = pl.multiple_of((1 - core) * shard, shard)
+    far = pl.ds((1 - core) * some, some)
+    near = pl.ds(core * some, some)
+    for p in range(GROUP):
+        rows = slice(p * ROWS, (p + 1) * ROWS)
+        q_ref[p, pl.ds(other, shard), :] = in_ref[far, rows, :].reshape(shard, DH)
+        rows = slice(KV_ROWS + p * ROWS, KV_ROWS + (p + 1) * ROWS)
+        q_ref[p, pl.ds(mine, shard), :] = swap_ref[:, rows, :].reshape(shard, DH)
+    for n, buf in enumerate((k_buf, v_buf)):
+        rows = slice(n * ROWS, (n + 1) * ROWS)
+        buf[pl.ds(mine, shard), :] = before_ref[:, rows, :].reshape(shard, DH)
+        buf[pl.ds(other, shard), :] = before_swap_ref[:, rows, :].reshape(shard, DH)
+        held = slice(KVNAT + n * ROWS, KVNAT + (n + 1) * ROWS)
+        buf[pl.ds(pair + mine, shard), :] = in_ref[near, held, :].reshape(shard, DH)
+        buf[pl.ds(pair + other, shard), :] = swap_ref[:, rows, :].reshape(shard, DH)
 
     first_block = meta[M_HI] * 8
     band = 8 * BLOCK
@@ -193,6 +197,7 @@
     k_buf,
     v_buf,
     stats_buf,
+    bias_buf,
 ):
     lo = meta[M_LO]
     g = lo >> 1
@@ -219,7 +224,11 @@
             v_buf[pl.ds(at, BLOCK), :] = all_ref[source, BLOCK : 2 * BLOCK, :]
             ids = jnp.where(of_lane == jnp.where(mine, count, NV), v, ids)
             count = count + mine.astype(jnp.int32)
-        mask = jnp.full((1, width), meta[M_MASK + head], jnp.int32)
+        block_of_row = lax.broadcasted_iota(jnp.int32, (8, width), 0) + first_block
+        distance = block_of_row - ids
+        mask = jnp.full((8, width), meta[M_MASK + head], jnp.int32)
+        slashed = jnp.right_shift(mask, jnp.clip(distance, 0, 31)) & 1
+        bias_buf[...] = jnp.where((distance > 0) & (slashed == 0), 0.0, -jnp.inf)
 
         def attend(n):
             size = n * BLOCK
@@ -231,9 +240,8 @@
                 s = scores(q_buf[p, span, :], k_buf[0:size, :])
                 parts = []
                 for t in range(rows // BLOCK):
-                    distance = first_block + i * (rows // BLOCK) + t - ids[:, 0:size]
-                    slashed = jnp.right_shift(mask[:, 0:size], jnp.clip(distance, 0, 31)) & 1
-                    bias = jnp.where((distance > 0) & (slashed == 0), 0.0, -jnp.inf)
+                    at = i * (rows // BLOCK) + t
+                    bias = bias_buf[at : at + 1, 0:size]
                     parts.append(s[t * BLOCK : (t + 1) * BLOCK] + bias)
                 s = jnp.concatenate(parts, axis=0)
                 top = jnp.maximum(jnp.max(s, axis=1, keepdims=True), LOWEST)
@@ -262,18 +270,26 @@
     second = stats.astype(bf16).astype(f32)
     third = stats - second
     packed = first + pltpu.roll(second, PART, 1) + pltpu.roll(third, 2 * PART, 1)
-    out_ref[:, STATS:, :] = packed.astype(bf16).reshape(LO, ROWS, DH)
+    packed = packed.reshape(LO, ROWS, DH)
+    low = packed[:, 0 : ROWS // 2, :].reshape(LO * ROWS // 2, DH)
+    high = packed[:, ROWS // 2 :, :].reshape(LO * ROWS // 2, DH)
+    packed = low + pltpu.roll(high, DH // 2, 1)
+    out_ref[:, STATS:, :] = packed.astype(bf16).reshape(LO, ROWS // 2, DH)
 
 
 def exit_kernel(meta, in_ref, gate_ref, out_ref, m_buf, l_buf):
     row = lax.broadcasted_iota(jnp.int32, (DH, SLOTS * DH), 0)
     col = lax.broadcasted_iota(jnp.int32, (DH, SLOTS * DH), 1) // DH
-    row = jnp.where(row < 3 * PART, row % PART, PART)
-    m_pick = jnp.where(row == col, 1.0, 0.0).astype(bf16)
-    l_pick = jnp.where(row == col + L_LANE, 1.0, 0.0).astype(bf16)
-    stats = in_ref[:, STATS:, :].reshape(LO * ROWS, DH)
-    m_buf[...] = jnp.dot(stats, m_pick, preferred_element_type=f32).reshape(LO, ROWS, SLOTS * DH)
-    l_buf[...] = jnp.dot(stats, l_pick, preferred_element_type=f32).reshape(LO, ROWS, SLOTS * DH)
+    stats = in_ref[:, STATS:, :].reshape(LO * ROWS // 2, DH)
+    for side in range(2):
+        at = row - side * (DH // 2)
+        value = jnp.where((at >= 0) & (at < 3 * PART), at & (PART - 1), PART)
+        held = slice(side * ROWS // 2, (side + 1) * ROWS // 2)
+        for buf, lane in ((m_buf, 0), (l_buf, L_LANE)):
+            pick = jnp.where(value == col + lane, 1.0, 0.0).astype(bf16)
+            buf[:, held, :] = jnp.dot(stats, pick, preferred_element_type=f32).reshape(
+                LO, ROWS // 2, SLOTS * DH
+            )
 
     def source_step(n, _):
         for a in range(2):
@@ -342,9 +358,13 @@
     mine = lax.all_to_all(sent, "lo", 0, 0, tiled=True)
     spread, swap, kv_own = call(
         pick_kernel,
-        (shape(2 * BLOCK, lead=HI), in_vmem(QNAT - QDYN), in_vmem(ROWS)),
-        [SMEM, SMEM, VMEM],
-    )(meta, vertical_blocks, mine)
+        (
+            shape(2 * BLOCK, lead=HI),
+            in_vmem(KV_ROWS + QNAT, lead=LO // 2),
+            in_vmem(KV_ROWS, lead=LO // 2),
+        ),
+        [SMEM, VMEM],
+    )(meta, mine)
     before = lax.ppermute(kv_own, ("y", "k"), [(i, i + 1) for i in range(HI - 1)])
     verticals = lax.all_to_all(spread, ("y", "k"), 0, 0, tiled=True)
     partner = [(i, i ^ 1) for i in range(LO)]
@@ -358,12 +378,13 @@
     )(meta, mine, swapped, before, before_swap)
     partial = call(
         vertical_kernel,
-        shape(OUT_ROWS),
+        in_vmem(OUT_ROWS),
         [SMEM, SMEM, LOADED, VMEM, LOADED, LOADED],
         [
             pltpu.VMEM(((NV + 1) * BLOCK, DH), bf16),
             pltpu.VMEM(((NV + 1) * BLOCK, DH), bf16),
             pltpu.VMEM((LO * ROWS, DH), f32),
+            pltpu.VMEM((8, NV * BLOCK), f32),
         ],
     )(meta, vertical_blocks, vertical_queries, verticals, slash, slash_stats)
     back = lax.all_to_all(partial, "lo", 0, 0, tiled=True)

time: 115 us -> 110 us (0.957)
  the two profiles are of different devices: /device:TPU:24 before, /device:TPU:8 now
where the time goes in v5:
time: 110 us
  waiting for transfers between devices  38.1 us (35%)
  starting transfers between devices  29.6 us (27%)
  blocking collectives  18.4 us (17%)
  Pallas kernels  17.1 us (16%)
  local copies, waits for them, and re-layouts  4.18 us (4%)
  other arithmetic  2.37 us (2%)
    ppermute x1, waiting for transfers between devices, body(): lax.ppermute(kv_own, ('y', 'k'), [(i, i + 1) for i in range(HI - 1)])  26.3 us
    all_to_all x1, blocking collectives, body(): back = lax.all_to_all(partial, 'lo', 0, 0, tiled=True)  18.4 us
    pallas_call x5, Pallas kernels, placed(): run(*(pltpu.with_memory_space_constraint(arg, pltpu.VMEM) if spec is VMEM...  17.1 us
    all_to_all x1, starting transfers between devices, body(): verticals = lax.all_to_all(spread, ('y', 'k'), 0, 0, tiled=True)  15.3 us
    all_to_all x1, waiting for transfers between devices, body(): mine = lax.all_to_all(sent, 'lo', 0, 0, tiled=True)  11.2 us
    all_to_all x1, starting transfers between devices, body(): mine = lax.all_to_all(sent, 'lo', 0, 0, tiled=True)  6.21 us
    ppermute x1, starting transfers between devices, body(): lax.ppermute(kv_own, ('y', 'k'), [(i, i + 1) for i in range(HI - 1)])  4.27 us
    unnamed x12, local copies, waits for them, and re-layouts  2.96 us
  transfers between devices with their start and end apart: 5, of which 3 were waited for; matrix products, arithmetic and copies ran while one was open for 2% of the time, Pallas kernels for 5%

profile of v5, /device:TPU:8, one launch (start us, length us, event | category | flops | bytes accessed | tf_op | source)
XLA Modules:
  0.0 109.8 jit_solution(5498690190591158048)
XLA Ops:
  0.0 0.7 iota_add_fusion
  0.7 0.2 convert_reduce_fusion
  1.0 0.9 copy.9
  2.0 0.7 copy-done.2
  2.7 0.1 select_reduce_fusion.1
  2.8 0.6 pad_add_fusion.meta
  3.4 1.7 %shard_map.64 = bf16[16,192,128]{2,1,0:T(8,128)(2,1)} custom-call(s32[41]{0:T(128)} %pad_add_fusion.meta, bf16[32,4096]{1,0:T(8,128)(2,1)S(1)} %copy-done.1, bf16[32,2048]{1,0:T(8,128)(2,1)S(1)} %bitcast.6), custom_call_target="tpu_custom_call" | custom-call | tf_op jit(solution)/shard_map/pallas_call | solution.py:336
  5.1 6.2 %all-to-all-start = ((bf16[16,192,128]{2,1,0:T(8,128)(2,1)}), bf16[16,192,128]{2,1,0:T(8,128)(2,1)S(1)}, u32[]{:S(2)}, u32[]{:S(2)}) async-start(bf16[16,192,128]{2,1,0:T(8,128)(2,1)} %shard_map.64), calls=%async_computation | async-start | bytes 1572864 | tf_op jit(solution)/shard_map/all_to_all | solution.py:358
  11.4 0.7 copy-done.3
  12.1 0.6 fusion.1
  12.7 1.2 %concatenate.6.meta = s32[99]{0:T(128)} concatenate(s32[32]{0:T(128)S(1)} %select_reduce_fusion, s32[32]{0:T(128)S(1)} %multiply_add_fusion, s32[32]{0:T(128)S(1)} %select_reduce_fusion.2, s32[1]{0:T(128)} %bitcast, s32[1]{0:T(128)} %bitcast.1, s32[1]{0:T(128)} %bitcast.2), dimensions={0} | concatenate | bytes 792 | tf_op jit(solution)/shard_map/concatenate | solution.py:68
  13.9 11.2 %all-to-all-done.in_ref = bf16[16,192,128]{2,1,0:T(8,128)(2,1)S(1)} async-done(((bf16[16,192,128]{2,1,0:T(8,128)(2,1)}), bf16[16,192,128]{2,1,0:T(8,128)(2,1)S(1)}, u32[]{:S(2)}, u32[]{:S(2)}) %all-to-all-start) | async-done | bytes 786464 | tf_op jit(solution)/shard_map/all_to_all | solution.py:358
  25.1 1.9 %shard_map.65 = (bf16[32,128,128]{2,1,0:T(8,128)(2,1)}, bf16[8,192,128]{2,1,0:T(8,128)(2,1)S(1)}, bf16[8,64,128]{2,1,0:T(8,128)(2,1)S(1)}) custom-call(s32[99]{0:T(128)} %concatenate.6.meta, bf16[16,192,128]{2,1,0:T(8,128)(2,1)S(1)} %all-to-all-done.in_ref), custom_call_target="tpu_custom_call" | custom-call | tf_op jit(solution)/shard_map/pallas_call | solution.py:336
  27.0 15.3 %all-to-all-start.1 = ((bf16[32,128,128]{2,1,0:T(8,128)(2,1)}), bf16[32,128,128]{2,1,0:T(8,128)(2,1)S(1)}, u32[]{:S(2)}, u32[]{:S(2)}) async-start(bf16[32,128,128]{2,1,0:T(8,128)(2,1)} %get-tuple-element.14), calls=%async_computation.1 | async-start | bytes 2097152 | tf_op jit(solution)/shard_map/all_to_all | solution.py:369
  42.3 1.9 %collective-permute-start = (bf16[8,192,128]{2,1,0:T(8,128)(2,1)S(1)}, bf16[8,192,128]{2,1,0:T(8,128)(2,1)S(1)}, u32[]{:S(2)}, u32[]{:S(2)}) collective-permute-start(bf16[8,192,128]{2,1,0:T(8,128)(2,1)S(1)} %get-tuple-element.11), channel_id=1, source_target_pairs={{0,1},{1,0},{2,3},{3,2},{4,5},{5,4},{6,7},{7,6},{8,9},{9,8},{10,11... | collective-permute-start | bytes 1179656 | tf_op jit(solution)/shard_map/ppermute | solution.py:371
  44.2 4.3 %collective-permute-start.1 = (bf16[8,64,128]{2,1,0:T(8,128)(2,1)S(1)}, bf16[8,64,128]{2,1,0:T(8,128)(2,1)S(1)}, u32[]{:S(2)}, u32[]{:S(2)}) collective-permute-start(bf16[8,64,128]{2,1,0:T(8,128)(2,1)S(1)} %get-tuple-element.12), channel_id=1, source_target_pairs={{0,16},{16,32},{32,48},{48,64},{64,80},{80,96},{96,112},{112,128},... | collective-permute-start | bytes 393224 | tf_op jit(solution)/shard_map/ppermute | solution.py:368
  48.5 26.3 %collective-permute-done.1.before_ref = bf16[8,64,128]{2,1,0:T(8,128)(2,1)S(1)} collective-permute-done((bf16[8,64,128]{2,1,0:T(8,128)(2,1)S(1)}, bf16[8,64,128]{2,1,0:T(8,128)(2,1)S(1)}, u32[]{:S(2)}, u32[]{:S(2)}) %collective-permute-start.1) | collective-permute-done | bytes 131104 | tf_op jit(solution)/shard_map/ppermute | solution.py:368
  74.8 1.9 %collective-permute-start.2 = (bf16[8,64,128]{2,1,0:T(8,128)(2,1)S(1)}, bf16[8,64,128]{2,1,0:T(8,128)(2,1)S(1)}, u32[]{:S(2)}, u32[]{:S(2)}) collective-permute-start(bf16[8,64,128]{2,1,0:T(8,128)(2,1)S(1)} %collective-permute-done.1.before_ref), channel_id=1, source_target_pairs={{0,1},{1,0},{2,3},{3,2},{4,5},{5,4},{6,7},{7,6},{8,9},{9,8},{10,11... | collective-permute-start | bytes 393224 | tf_op jit(solution)/shard_map/ppermute | solution.py:372
  76.7 0.7 copy.8.vert_ref
  77.4 0.6 collective-permute-done.2.before_swap_ref
  78.0 5.4 %shard_map.66 = (bf16[16,64,128]{2,1,0:T(8,128)(2,1)}, f32[16,32,128]{2,1,0:T(8,128)}, bf16[4,512,128]{2,1,0:T(8,128)(2,1)}) custom-call(s32[99]{0:T(128)} %concatenate.6.meta, bf16[16,192,128]{2,1,0:T(8,128)(2,1)S(1)} %all-to-all-done.in_ref, bf16[8,192,128]{2,1,0:T(8,128)(2,1)S(1)} %collective-permute-done.swap_ref, ...), custom_call_target="tpu_custom_call" | custom-call | tf_op jit(solution)/shard_map/pallas_call | solution.py:336
  83.4 5.3 %shard_map.67 = bf16[16,208,128]{2,1,0:T(8,128)(2,1)S(1)} custom-call(s32[99]{0:T(128)} %concatenate.6.meta, s32[32,16]{1,0:T(8,128)} %copy.8.vert_ref, bf16[4,512,128]{2,1,0:T(8,128)(2,1)} %get-tuple-element.13.q_buf, bf16[32,128,128]{2,1,0:T(8,128)(2,1)S(1)} %all-to-all-done.1.all_ref, bf16[16,64,128]{2,1,0:T(8,128)(2,1)} %get-tuple-element.15.slash_ref, ...), custom_call_target="tpu_custom_call" | custom-call | tf_op jit(solution)/shard_map/pallas_call | solution.py:336
  88.8 18.4 %all_to_all.15.in_ref = bf16[16,208,128]{2,1,0:T(8,128)(2,1)S(1)} all-to-all(bf16[16,208,128]{2,1,0:T(8,128)(2,1)S(1)} %shard_map.67), channel_id=1, replica_groups=mesh['y'=8,'k'=4,'lo'=16] {'lo'}, dimensions={0} | all-to-all | bytes 1703936 | tf_op jit(solution)/shard_map/all_to_all | solution.py:390
  107.1 2.7 %shard_map.68 = bf16[32,4096]{1,0:T(8,128)(2,1)} custom-call(s32[99]{0:T(128)} %concatenate.6.meta, bf16[16,208,128]{2,1,0:T(8,128)(2,1)S(1)} %all_to_all.15.in_ref, bf16[32,4096]{1,0:T(8,128)(2,1)S(1)} %copy-done), custom_call_target="tpu_custom_call" | custom-call | tf_op jit(solution)/shard_map/pallas_call | solution.py:336
  (16 shorter events, 0.2 us)
Async XLA Ops:
  0.0 3.4 %copy-start.1 = (bf16[32,4096]{1,0:T(8,128)(2,1)S(1)}, bf16[32,4096]{1,0:T(8,128)(2,1)}, u32[]{:S(2)}) copy-start(bf16[32,4096]{1,0:T(8,128)(2,1)} %q_ref.1) | copy-start | bytes 786436
  2.0 0.7 copy-start.2
  5.1 19.9 %all-to-all-start = ((bf16[16,192,128]{2,1,0:T(8,128)(2,1)}), bf16[16,192,128]{2,1,0:T(8,128)(2,1)S(1)}, u32[]{:S(2)}, u32[]{:S(2)}) async-start(bf16[16,192,128]{2,1,0:T(8,128)(2,1)} %shard_map.64), calls=%async_computation | async-start | bytes 1572864 | tf_op jit(solution)/shard_map/all_to_all | solution.py:358
  11.4 0.7 copy-start.3
  11.4 0.7 copy-start.4
  27.0 56.4 %all-to-all-start.1 = ((bf16[32,128,128]{2,1,0:T(8,128)(2,1)}), bf16[32,128,128]{2,1,0:T(8,128)(2,1)S(1)}, u32[]{:S(2)}, u32[]{:S(2)}) async-start(bf16[32,128,128]{2,1,0:T(8,128)(2,1)} %get-tuple-element.14), calls=%async_computation.1 | async-start | bytes 2097152 | tf_op jit(solution)/shard_map/all_to_all | solution.py:369
  42.3 35.7 %collective-permute-start = (bf16[8,192,128]{2,1,0:T(8,128)(2,1)S(1)}, bf16[8,192,128]{2,1,0:T(8,128)(2,1)S(1)}, u32[]{:S(2)}, u32[]{:S(2)}) collective-permute-start(bf16[8,192,128]{2,1,0:T(8,128)(2,1)S(1)} %get-tuple-element.11), channel_id=1, source_target_pairs={{0,1},{1,0},{2,3},{3,2},{4,5},{5,4},{6,7},{7,6},{8,9},{9,8},{10,11... | collective-permute-start | bytes 1179656 | tf_op jit(solution)/shard_map/ppermute | solution.py:371
  44.2 30.5 %collective-permute-start.1 = (bf16[8,64,128]{2,1,0:T(8,128)(2,1)S(1)}, bf16[8,64,128]{2,1,0:T(8,128)(2,1)S(1)}, u32[]{:S(2)}, u32[]{:S(2)}) collective-permute-start(bf16[8,64,128]{2,1,0:T(8,128)(2,1)S(1)} %get-tuple-element.12), channel_id=1, source_target_pairs={{0,16},{16,32},{32,48},{48,64},{64,80},{80,96},{96,112},{112,128},... | collective-permute-start | bytes 393224 | tf_op jit(solution)/shard_map/ppermute | solution.py:368
  74.8 3.2 %collective-permute-start.2 = (bf16[8,64,128]{2,1,0:T(8,128)(2,1)S(1)}, bf16[8,64,128]{2,1,0:T(8,128)(2,1)S(1)}, u32[]{:S(2)}, u32[]{:S(2)}) collective-permute-start(bf16[8,64,128]{2,1,0:T(8,128)(2,1)S(1)} %collective-permute-done.1.before_ref), channel_id=1, source_target_pairs={{0,1},{1,0},{2,3},{3,2},{4,5},{5,4},{6,7},{7,6},{8,9},{9,8},{10,11... | collective-permute-start | bytes 393224 | tf_op jit(solution)/shard_map/ppermute | solution.py:372
  88.8 18.4 %copy-start = (bf16[32,4096]{1,0:T(8,128)(2,1)S(1)}, bf16[32,4096]{1,0:T(8,128)(2,1)}, u32[]{:S(2)}) copy-start(bf16[32,4096]{1,0:T(8,128)(2,1)} %gate_ref.1) | copy-start | bytes 786436

commit v6 on v5

--- a/solution.py
+++ b/solution.py
@@ -29,7 +29,6 @@
 L_LANE = 8
 PART = 16
 M_HEAD, M_SLOT, M_MASK, M_HI, M_LO, M_BLOCK = 0, 32, 64, 96, 97, 98
-E_HEAD, E_KV, E_ZL = 0, 32, 40
 
 bf16 = jnp.bfloat16
 f32 = jnp.float32
@@ -52,35 +51,57 @@
     head_of = jnp.sum(jnp.where(slot[None, :] == heads[:, None], heads[None, :], 0), axis=1)
     live = jnp.arange(NS, dtype=jnp.int32)[None, :] < slash_count[:, None]
     mask = jnp.sum(jnp.where(live, jnp.left_shift(1, slash_offsets), 0), axis=1)
-    shard = hi * 2 + lo // (LO // 2)
-    here = jnp.any(vertical_blocks // 4 == shard, axis=1)
-    kv_of = jnp.sum(
-        jnp.where(
-            (group[None, :] == jnp.arange(groups, dtype=jnp.int32)[:, None]) & here[None, :],
-            (heads // (H // KVH))[None, :],
-            0,
-        ),
-        axis=1,
-    )
     taken = (group == lo // 2)[:, None] & (vertical_blocks // 4 == hi * 2 + lo % 2)
     block = jnp.sum(jnp.where(taken, vertical_blocks % 4, 0))
-    entry = jnp.concatenate([head_of, kv_of, (lo // (LO // 2))[None]]).astype(jnp.int32)
     rest = jnp.concatenate([head_of, slot, mask, jnp.stack([hi, lo, block])])
-    return entry, rest.astype(jnp.int32)
-
-
-def entry_kernel(meta, q_ref, kv_ref, out_ref):
+    return rest.astype(jnp.int32)
+
+
+def entry_tables(count_ref, vert_ref, shard, start, head_of, kv_of):
+    head = lax.broadcasted_iota(jnp.int32, vert_ref.shape, 1)
+    weight = jnp.left_shift(1, head & 15).astype(f32)
+    hit = jnp.where((vert_ref[...] >> 2) == shard, weight, 0.0)
+    here = [
+        jnp.sum(jnp.where((head >> 4) == part, hit, 0.0)).astype(jnp.int32) for part in range(2)
+    ]
+    for n in range(NS + 1):
+        start[n] = 0
+    for h in range(H):
+        start[count_ref[h]] = start[count_ref[h]] + 1
+    before = jnp.int32(0)
+    for n in range(NS + 1):
+        held = start[n]
+        start[n] = before
+        before = before + held
+    groups = H // GROUP
+    for h in range(H):
+        rank = start[count_ref[h]]
+        start[count_ref[h]] = rank + 1
+        within = rank >> 3
+        place = rank & (groups - 1)
+        group = jnp.where((within & 1) == 0, place, groups - 1 - place)
+        head_of[group * GROUP + within] = h
+        kv_of[jnp.where(((here[h >> 4] >> (h & 15)) & 1) == 1, group, groups)] = h // (H // KVH)
+
+
+def entry_kernel(count_ref, vert_ref, q_ref, kv_ref, out_ref, start, head_of, kv_of):
+    lo = lax.axis_index("lo")
+    zl = lo >> 3
+    shard = (lax.axis_index("y") * NK + lax.axis_index("k")) * 2 + zl
+    for g in range(KVH):
+        kv_of[g] = 0
+    entry_tables(count_ref, vert_ref, shard, start, head_of, kv_of)
+
     def q_cols(head):
         return q_ref[:, pl.ds(pl.multiple_of(head * DH, DH), DH)]
 
     def kv_cols(which, head):
         return kv_ref[:, pl.ds(pl.multiple_of(which * KVH * DH + head * DH, DH), DH)]
 
-    zl = meta[E_ZL]
     for g in range(KVH):
-        kv_head = meta[E_KV + g]
+        kv_head = kv_of[g]
         near = [kv_cols(0, kv_head), kv_cols(1, kv_head), kv_cols(0, g), kv_cols(1, g)]
-        far = [q_cols(meta[E_HEAD + g * GROUP + p]) for p in range(GROUP)]
+        far = [q_cols(head_of[g * GROUP + p]) for p in range(GROUP)]
         for core, parts in ((zl, near), (1 - zl, far)):
             own = [q_cols(4 * g + 2 * core + a) for a in range(2)]
             for n, part in enumerate(parts + own):
@@ -216,7 +237,7 @@
         count = jnp.int32(0)
         ids = jnp.full((1, width), 1 << 20, jnp.int32)
         for j in range(NV):
-            v = vert_ref[head, j]
+            v = vert_ref[j, head]
             mine = ((v >> 2) & 1) == c
             source = v >> 3
             at = pl.multiple_of(count * BLOCK, BLOCK)
@@ -291,7 +312,7 @@
                 LO, ROWS // 2, SLOTS * DH
             )
 
-    def source_step(n, _):
+    for n in range(LO):
         for a in range(2):
             h = 2 * n + a
             cols = slice((GROUP + a) * DH, (GROUP + a + 1) * DH)
@@ -314,12 +335,9 @@
                 num = num + w * acc.astype(f32)
                 den = den + w * total
             attended = (num / den).astype(bf16).astype(f32)
-            at = pl.ds(pl.multiple_of(h * DH, DH), DH)
+            at = slice(h * DH, (h + 1) * DH)
             gate = gate_ref[:, at].astype(f32)
             out_ref[:, at] = (jax.nn.sigmoid(gate) * attended).astype(bf16)
-        return 0
-
-    lax.fori_loop(0, LO, source_step, 0, unroll=2)
 
 
 def call(kernel, out_shape, in_specs, scratch=(), **options):
@@ -352,9 +370,15 @@
 
 
 def body(queries, key_values, gate_logits, vertical_blocks, slash_offsets, slash_count):
-    entry_meta, meta = tables(vertical_blocks, slash_offsets, slash_count)
+    meta = tables(vertical_blocks, slash_offsets, slash_count)
+    vertical_ids = vertical_blocks.T
     flat_kv = key_values.reshape(ROWS, 2 * KVH * DH)
-    sent = call(entry_kernel, shape(IN_ROWS), [SMEM, VMEM, VMEM])(entry_meta, queries, flat_kv)
+    sent = call(
+        entry_kernel,
+        shape(IN_ROWS),
+        [SMEM, LOADED, VMEM, VMEM],
+        [pltpu.SMEM((16,), jnp.int32), pltpu.SMEM((H,), jnp.int32), pltpu.SMEM((16,), jnp.int32)],
+    )(slash_count, vertical_ids, queries, flat_kv)
     mine = lax.all_to_all(sent, "lo", 0, 0, tiled=True)
     spread, swap, kv_own = call(
         pick_kernel,
@@ -386,7 +410,7 @@
             pltpu.VMEM((LO * ROWS, DH), f32),
             pltpu.VMEM((8, NV * BLOCK), f32),
         ],
-    )(meta, vertical_blocks, vertical_queries, verticals, slash, slash_stats)
+    )(meta, vertical_ids, vertical_queries, verticals, slash, slash_stats)
     back = lax.all_to_all(partial, "lo", 0, 0, tiled=True)
     return call(
         exit_kernel,

time: 110 us -> 108 us (0.982)
  other arithmetic: 2.37 us -> 1.04 us
    unnamed x12 -> x11, local copies, waits for them, and re-layouts: 2.96 us -> 2.03 us
where the time goes in v6:
time: 108 us
  waiting for transfers between devices  37.9 us (35%)
  starting transfers between devices  29.6 us (27%)
  blocking collectives  18.3 us (17%)
  Pallas kernels  17.3 us (16%)
  local copies, waits for them, and re-layouts  3.32 us (3%)
    ppermute x1, waiting for transfers between devices, body(): lax.ppermute(kv_own, ('y', 'k'), [(i, i + 1) for i in range(HI - 1)])  26.3 us
    all_to_all x1, blocking collectives, body(): back = lax.all_to_all(partial, 'lo', 0, 0, tiled=True)  18.3 us
    pallas_call x5, Pallas kernels, placed(): run(*(pltpu.with_memory_space_constraint(arg, pltpu.VMEM) if spec is VMEM...  17.3 us
    all_to_all x1, starting transfers between devices, body(): verticals = lax.all_to_all(spread, ('y', 'k'), 0, 0, tiled=True)  15.3 us
    all_to_all x1, waiting for transfers between devices, body(): mine = lax.all_to_all(sent, 'lo', 0, 0, tiled=True)  10.3 us
    all_to_all x1, starting transfers between devices, body(): mine = lax.all_to_all(sent, 'lo', 0, 0, tiled=True)  6.21 us
    ppermute x1, starting transfers between devices, body(): lax.ppermute(kv_own, ('y', 'k'), [(i, i + 1) for i in range(HI - 1)])  4.27 us
  transfers between devices with their start and end apart: 5, of which 3 were waited for; matrix products, arithmetic and copies ran while one was open for 2% of the time, Pallas kernels for 5%

profile of v6, /device:TPU:8, one launch (start us, length us, event | category | flops | bytes accessed | tf_op | source)
XLA Modules:
  0.0 107.6 jit_solution(13584293072874603869)
XLA Ops:
  0.0 1.0 copy.7
  1.0 0.0 copy-done.1
  1.0 2.1 %shard_map.64 = bf16[16,192,128]{2,1,0:T(8,128)(2,1)} custom-call(s32[32]{0:T(128)} %count_ref.1, s32[16,32]{1,0:T(8,128)} %bitcast.8, bf16[32,4096]{1,0:T(8,128)(2,1)S(1)} %copy-done.1, bf16[32,2048]{1,0:T(8,128)(2,1)S(1)} %bitcast.6), custom_call_target="tpu_custom_call" | custom-call | tf_op jit(solution)/shard_map/pallas_call | solution.py:354
  3.1 6.2 %all-to-all-start = ((bf16[16,192,128]{2,1,0:T(8,128)(2,1)}), bf16[16,192,128]{2,1,0:T(8,128)(2,1)S(1)}, u32[]{:S(2)}, u32[]{:S(2)}) async-start(bf16[16,192,128]{2,1,0:T(8,128)(2,1)} %shard_map.64), calls=%async_computation | async-start | bytes 1572864 | tf_op jit(solution)/shard_map/all_to_all | solution.py:382
  9.4 0.0 copy-start.3
  9.4 0.0 copy-start.4
  9.4 0.7 copy-done.3
  10.1 0.2 convert_reduce_fusion
  10.3 0.1 select_reduce_fusion
  10.4 0.3 copy-done.2
  10.8 0.7 fusion.2
  11.5 1.3 %concatenate.3.meta = s32[99]{0:T(128)} concatenate(s32[32]{0:T(128)S(1)} %select_reduce_fusion, s32[32]{0:T(128)S(1)} %multiply_add_fusion, s32[32]{0:T(128)S(1)} %select_reduce_fusion.1, s32[1]{0:T(128)} %bitcast, s32[1]{0:T(128)} %bitcast.1, s32[1]{0:T(128)} %bitcast.2), dimensions={0} | concatenate | bytes 792 | tf_op jit(solution)/shard_map/concatenate | solution.py:56
  12.8 10.3 %all-to-all-done.in_ref = bf16[16,192,128]{2,1,0:T(8,128)(2,1)S(1)} async-done(((bf16[16,192,128]{2,1,0:T(8,128)(2,1)}), bf16[16,192,128]{2,1,0:T(8,128)(2,1)S(1)}, u32[]{:S(2)}, u32[]{:S(2)}) %all-to-all-start) | async-done | bytes 786464 | tf_op jit(solution)/shard_map/all_to_all | solution.py:382
  23.1 1.9 %shard_map.65 = (bf16[32,128,128]{2,1,0:T(8,128)(2,1)}, bf16[8,192,128]{2,1,0:T(8,128)(2,1)S(1)}, bf16[8,64,128]{2,1,0:T(8,128)(2,1)S(1)}) custom-call(s32[99]{0:T(128)} %concatenate.3.meta, bf16[16,192,128]{2,1,0:T(8,128)(2,1)S(1)} %all-to-all-done.in_ref), custom_call_target="tpu_custom_call" | custom-call | tf_op jit(solution)/shard_map/pallas_call | solution.py:354
  25.0 15.3 %all-to-all-start.1 = ((bf16[32,128,128]{2,1,0:T(8,128)(2,1)}), bf16[32,128,128]{2,1,0:T(8,128)(2,1)S(1)}, u32[]{:S(2)}, u32[]{:S(2)}) async-start(bf16[32,128,128]{2,1,0:T(8,128)(2,1)} %get-tuple-element.14), calls=%async_computation.1 | async-start | bytes 2097152 | tf_op jit(solution)/shard_map/all_to_all | solution.py:393
  40.3 1.9 %collective-permute-start = (bf16[8,192,128]{2,1,0:T(8,128)(2,1)S(1)}, bf16[8,192,128]{2,1,0:T(8,128)(2,1)S(1)}, u32[]{:S(2)}, u32[]{:S(2)}) collective-permute-start(bf16[8,192,128]{2,1,0:T(8,128)(2,1)S(1)} %get-tuple-element.11), channel_id=1, source_target_pairs={{0,1},{1,0},{2,3},{3,2},{4,5},{5,4},{6,7},{7,6},{8,9},{9,8},{10,11... | collective-permute-start | bytes 1179656 | tf_op jit(solution)/shard_map/ppermute | solution.py:395
  42.2 4.3 %collective-permute-start.1 = (bf16[8,64,128]{2,1,0:T(8,128)(2,1)S(1)}, bf16[8,64,128]{2,1,0:T(8,128)(2,1)S(1)}, u32[]{:S(2)}, u32[]{:S(2)}) collective-permute-start(bf16[8,64,128]{2,1,0:T(8,128)(2,1)S(1)} %get-tuple-element.12), channel_id=1, source_target_pairs={{0,16},{16,32},{32,48},{48,64},{64,80},{80,96},{96,112},{112,128},... | collective-permute-start | bytes 393224 | tf_op jit(solution)/shard_map/ppermute | solution.py:392
  46.5 26.3 %collective-permute-done.1.before_ref = bf16[8,64,128]{2,1,0:T(8,128)(2,1)S(1)} collective-permute-done((bf16[8,64,128]{2,1,0:T(8,128)(2,1)S(1)}, bf16[8,64,128]{2,1,0:T(8,128)(2,1)S(1)}, u32[]{:S(2)}, u32[]{:S(2)}) %collective-permute-start.1) | collective-permute-done | bytes 131104 | tf_op jit(solution)/shard_map/ppermute | solution.py:392
  72.7 1.9 %collective-permute-start.2 = (bf16[8,64,128]{2,1,0:T(8,128)(2,1)S(1)}, bf16[8,64,128]{2,1,0:T(8,128)(2,1)S(1)}, u32[]{:S(2)}, u32[]{:S(2)}) collective-permute-start(bf16[8,64,128]{2,1,0:T(8,128)(2,1)S(1)} %collective-permute-done.1.before_ref), channel_id=1, source_target_pairs={{0,1},{1,0},{2,3},{3,2},{4,5},{5,4},{6,7},{7,6},{8,9},{9,8},{10,11... | collective-permute-start | bytes 393224 | tf_op jit(solution)/shard_map/ppermute | solution.py:396
  74.7 1.3 %collective-permute-done.2.before_swap_ref = bf16[8,64,128]{2,1,0:T(8,128)(2,1)S(1)} collective-permute-done((bf16[8,64,128]{2,1,0:T(8,128)(2,1)S(1)}, bf16[8,64,128]{2,1,0:T(8,128)(2,1)S(1)}, u32[]{:S(2)}, u32[]{:S(2)}) %collective-permute-start.2) | collective-permute-done | bytes 131104 | tf_op jit(solution)/shard_map/ppermute | solution.py:396
  76.0 5.4 %shard_map.66 = (bf16[16,64,128]{2,1,0:T(8,128)(2,1)}, f32[16,32,128]{2,1,0:T(8,128)}, bf16[4,512,128]{2,1,0:T(8,128)(2,1)}) custom-call(s32[99]{0:T(128)} %concatenate.3.meta, bf16[16,192,128]{2,1,0:T(8,128)(2,1)S(1)} %all-to-all-done.in_ref, bf16[8,192,128]{2,1,0:T(8,128)(2,1)S(1)} %collective-permute-done.swap_ref, ...), custom_call_target="tpu_custom_call" | custom-call | tf_op jit(solution)/shard_map/pallas_call | solution.py:354
  81.4 5.4 %shard_map.67 = bf16[16,208,128]{2,1,0:T(8,128)(2,1)S(1)} custom-call(s32[99]{0:T(128)} %concatenate.3.meta, s32[16,32]{1,0:T(8,128)} %bitcast.9, bf16[4,512,128]{2,1,0:T(8,128)(2,1)} %get-tuple-element.13.q_buf, bf16[32,128,128]{2,1,0:T(8,128)(2,1)S(1)} %all-to-all-done.1.all_ref, bf16[16,64,128]{2,1,0:T(8,128)(2,1)} %get-tuple-element.15.slash_ref, ...), custom_call_target="tpu_custom_call" | custom-call | tf_op jit(solution)/shard_map/pallas_call | solution.py:354
  86.8 18.3 %all_to_all.15.in_ref = bf16[16,208,128]{2,1,0:T(8,128)(2,1)S(1)} all-to-all(bf16[16,208,128]{2,1,0:T(8,128)(2,1)S(1)} %shard_map.67), channel_id=1, replica_groups=mesh['y'=8,'k'=4,'lo'=16] {'lo'}, dimensions={0} | all-to-all | bytes 1703936 | tf_op jit(solution)/shard_map/all_to_all | solution.py:414
  105.1 2.4 %shard_map.68 = bf16[32,4096]{1,0:T(8,128)(2,1)} custom-call(s32[99]{0:T(128)} %concatenate.3.meta, bf16[16,208,128]{2,1,0:T(8,128)(2,1)S(1)} %all_to_all.15.in_ref, bf16[32,4096]{1,0:T(8,128)(2,1)S(1)} %copy-done), custom_call_target="tpu_custom_call" | custom-call | tf_op jit(solution)/shard_map/pallas_call | solution.py:354
  (11 shorter events, 0.1 us)
Async XLA Ops:
  0.0 1.0 copy-start.1
  3.1 19.9 %all-to-all-start = ((bf16[16,192,128]{2,1,0:T(8,128)(2,1)}), bf16[16,192,128]{2,1,0:T(8,128)(2,1)S(1)}, u32[]{:S(2)}, u32[]{:S(2)}) async-start(bf16[16,192,128]{2,1,0:T(8,128)(2,1)} %shard_map.64), calls=%async_computation | async-start | bytes 1572864 | tf_op jit(solution)/shard_map/all_to_all | solution.py:382
  9.4 0.7 copy-start.3
  9.4 0.7 copy-start.4
  10.1 0.7 copy-start.2
  25.0 56.4 %all-to-all-start.1 = ((bf16[32,128,128]{2,1,0:T(8,128)(2,1)}), bf16[32,128,128]{2,1,0:T(8,128)(2,1)S(1)}, u32[]{:S(2)}, u32[]{:S(2)}) async-start(bf16[32,128,128]{2,1,0:T(8,128)(2,1)} %get-tuple-element.14), calls=%async_computation.1 | async-start | bytes 2097152 | tf_op jit(solution)/shard_map/all_to_all | solution.py:393
  40.3 35.7 %collective-permute-start = (bf16[8,192,128]{2,1,0:T(8,128)(2,1)S(1)}, bf16[8,192,128]{2,1,0:T(8,128)(2,1)S(1)}, u32[]{:S(2)}, u32[]{:S(2)}) collective-permute-start(bf16[8,192,128]{2,1,0:T(8,128)(2,1)S(1)} %get-tuple-element.11), channel_id=1, source_target_pairs={{0,1},{1,0},{2,3},{3,2},{4,5},{5,4},{6,7},{7,6},{8,9},{9,8},{10,11... | collective-permute-start | bytes 1179656 | tf_op jit(solution)/shard_map/ppermute | solution.py:395
  42.2 30.5 %collective-permute-start.1 = (bf16[8,64,128]{2,1,0:T(8,128)(2,1)S(1)}, bf16[8,64,128]{2,1,0:T(8,128)(2,1)S(1)}, u32[]{:S(2)}, u32[]{:S(2)}) collective-permute-start(bf16[8,64,128]{2,1,0:T(8,128)(2,1)S(1)} %get-tuple-element.12), channel_id=1, source_target_pairs={{0,16},{16,32},{32,48},{48,64},{64,80},{80,96},{96,112},{112,128},... | collective-permute-start | bytes 393224 | tf_op jit(solution)/shard_map/ppermute | solution.py:392
  72.7 3.2 %collective-permute-start.2 = (bf16[8,64,128]{2,1,0:T(8,128)(2,1)S(1)}, bf16[8,64,128]{2,1,0:T(8,128)(2,1)S(1)}, u32[]{:S(2)}, u32[]{:S(2)}) collective-permute-start(bf16[8,64,128]{2,1,0:T(8,128)(2,1)S(1)} %collective-permute-done.1.before_ref), channel_id=1, source_target_pairs={{0,1},{1,0},{2,3},{3,2},{4,5},{5,4},{6,7},{7,6},{8,9},{9,8},{10,11... | collective-permute-start | bytes 393224 | tf_op jit(solution)/shard_map/ppermute | solution.py:396
  86.8 18.3 %copy-start = (bf16[32,4096]{1,0:T(8,128)(2,1)S(1)}, bf16[32,4096]{1,0:T(8,128)(2,1)}, u32[]{:S(2)}) copy-start(bf16[32,4096]{1,0:T(8,128)(2,1)} %gate_ref.1) | copy-start | bytes 786436

commit v7 on v6

--- a/solution.py
+++ b/solution.py
@@ -19,7 +19,7 @@
 HI = NY * NK
 GROUP = 4
 LOWEST = -3.0e38
-STEPS = 2
+STEPS = 4
 EXP2_SCALE = DH**-0.5 * 1.4426950408889634
 
 VERT, KVNAT, QDYN, QNAT, IN_ROWS = 0, 64, 0, 128, 192
@@ -299,16 +299,17 @@
 
 
 def exit_kernel(meta, in_ref, gate_ref, out_ref, m_buf, l_buf):
-    row = lax.broadcasted_iota(jnp.int32, (DH, SLOTS * DH), 0)
-    col = lax.broadcasted_iota(jnp.int32, (DH, SLOTS * DH), 1) // DH
+    row = lax.broadcasted_iota(jnp.int32, (DH, DH), 0)
+    value = jnp.where(row < 3 * PART, row & (PART - 1), PART)
     stats = in_ref[:, STATS:, :].reshape(LO * ROWS // 2, DH)
-    for side in range(2):
-        at = row - side * (DH // 2)
-        value = jnp.where((at >= 0) & (at < 3 * PART), at & (PART - 1), PART)
-        held = slice(side * ROWS // 2, (side + 1) * ROWS // 2)
-        for buf, lane in ((m_buf, 0), (l_buf, L_LANE)):
-            pick = jnp.where(value == col + lane, 1.0, 0.0).astype(bf16)
-            buf[:, held, :] = jnp.dot(stats, pick, preferred_element_type=f32).reshape(
+    turned = pltpu.roll(stats.astype(f32), DH // 2, 1).astype(bf16)
+    for buf, lane in ((m_buf, 0), (l_buf, L_LANE)):
+        pick = jnp.concatenate(
+            [jnp.where(value == lane + n, 1.0, 0.0).astype(bf16) for n in range(SLOTS)], axis=1
+        )
+        for side, part in enumerate((stats, turned)):
+            held = slice(side * ROWS // 2, (side + 1) * ROWS // 2)
+            buf[:, held, :] = jnp.dot(part, pick, preferred_element_type=f32).reshape(
                 LO, ROWS // 2, SLOTS * DH
             )
 

time: 108 us -> 110 us (1.019)
  Pallas kernels: 17.3 us -> 18.9 us
    pallas_call x5, Pallas kernels: 17.3 us -> 18.9 us  [placed(): run(*(pltpu.with_memory_space_constraint(arg, pltpu.VMEM) if spec is VMEM...]
where the time goes in v7:
time: 110 us; the launch traced here: 109 us
  waiting for transfers between devices  37.9 us (34%)
  starting transfers between devices  29.6 us (27%)
  Pallas kernels  18.9 us (17%)
  blocking collectives  18.4 us (17%)
  local copies, waits for them, and re-layouts  3.32 us (3%)
    ppermute x1, waiting for transfers between devices, body(): lax.ppermute(kv_own, ('y', 'k'), [(i, i + 1) for i in range(HI - 1)])  26.3 us
    pallas_call x5, Pallas kernels, placed(): run(*(pltpu.with_memory_space_constraint(arg, pltpu.VMEM) if spec is VMEM...  18.9 us
    all_to_all x1, blocking collectives, body(): back = lax.all_to_all(partial, 'lo', 0, 0, tiled=True)  18.4 us
    all_to_all x1, starting transfers between devices, body(): verticals = lax.all_to_all(spread, ('y', 'k'), 0, 0, tiled=True)  15.3 us
    all_to_all x1, waiting for transfers between devices, body(): mine = lax.all_to_all(sent, 'lo', 0, 0, tiled=True)  10.3 us
    all_to_all x1, starting transfers between devices, body(): mine = lax.all_to_all(sent, 'lo', 0, 0, tiled=True)  6.21 us
    ppermute x1, starting transfers between devices, body(): lax.ppermute(kv_own, ('y', 'k'), [(i, i + 1) for i in range(HI - 1)])  4.27 us
  transfers between devices with their start and end apart: 5, of which 3 were waited for; matrix products, arithmetic and copies ran while one was open for 2% of the time, Pallas kernels for 5%

profile of v7, /device:TPU:8, one launch (start us, length us, event | category | flops | bytes accessed | tf_op | source)
XLA Modules:
  0.0 109.2 jit_solution(8248223643371087871)
XLA Ops:
  0.0 1.0 copy.7
  1.0 0.0 copy-done.1
  1.0 2.1 %shard_map.64 = bf16[16,192,128]{2,1,0:T(8,128)(2,1)} custom-call(s32[32]{0:T(128)} %count_ref.1, s32[16,32]{1,0:T(8,128)} %bitcast.8, bf16[32,4096]{1,0:T(8,128)(2,1)S(1)} %copy-done.1, bf16[32,2048]{1,0:T(8,128)(2,1)S(1)} %bitcast.6), custom_call_target="tpu_custom_call" | custom-call | tf_op jit(solution)/shard_map/pallas_call | solution.py:355
  3.1 6.2 %all-to-all-start = ((bf16[16,192,128]{2,1,0:T(8,128)(2,1)}), bf16[16,192,128]{2,1,0:T(8,128)(2,1)S(1)}, u32[]{:S(2)}, u32[]{:S(2)}) async-start(bf16[16,192,128]{2,1,0:T(8,128)(2,1)} %shard_map.64), calls=%async_computation | async-start | bytes 1572864 | tf_op jit(solution)/shard_map/all_to_all | solution.py:383
  9.4 0.0 copy-start.3
  9.4 0.7 copy-done.3
  10.1 0.2 convert_reduce_fusion
  10.3 0.1 select_reduce_fusion
  10.4 0.3 copy-done.2
  10.8 0.7 fusion.2
  11.5 1.3 %concatenate.3.meta = s32[99]{0:T(128)} concatenate(s32[32]{0:T(128)S(1)} %select_reduce_fusion, s32[32]{0:T(128)S(1)} %multiply_add_fusion, s32[32]{0:T(128)S(1)} %select_reduce_fusion.1, s32[1]{0:T(128)} %bitcast, s32[1]{0:T(128)} %bitcast.1, s32[1]{0:T(128)} %bitcast.2), dimensions={0} | concatenate | bytes 792 | tf_op jit(solution)/shard_map/concatenate | solution.py:56
  12.8 10.3 %all-to-all-done.in_ref = bf16[16,192,128]{2,1,0:T(8,128)(2,1)S(1)} async-done(((bf16[16,192,128]{2,1,0:T(8,128)(2,1)}), bf16[16,192,128]{2,1,0:T(8,128)(2,1)S(1)}, u32[]{:S(2)}, u32[]{:S(2)}) %all-to-all-start) | async-done | bytes 786464 | tf_op jit(solution)/shard_map/all_to_all | solution.py:383
  23.1 1.9 %shard_map.65 = (bf16[32,128,128]{2,1,0:T(8,128)(2,1)}, bf16[8,192,128]{2,1,0:T(8,128)(2,1)S(1)}, bf16[8,64,128]{2,1,0:T(8,128)(2,1)S(1)}) custom-call(s32[99]{0:T(128)} %concatenate.3.meta, bf16[16,192,128]{2,1,0:T(8,128)(2,1)S(1)} %all-to-all-done.in_ref), custom_call_target="tpu_custom_call" | custom-call | tf_op jit(solution)/shard_map/pallas_call | solution.py:355
  25.0 15.3 %all-to-all-start.1 = ((bf16[32,128,128]{2,1,0:T(8,128)(2,1)}), bf16[32,128,128]{2,1,0:T(8,128)(2,1)S(1)}, u32[]{:S(2)}, u32[]{:S(2)}) async-start(bf16[32,128,128]{2,1,0:T(8,128)(2,1)} %get-tuple-element.14), calls=%async_computation.1 | async-start | bytes 2097152 | tf_op jit(solution)/shard_map/all_to_all | solution.py:394
  40.3 1.9 %collective-permute-start = (bf16[8,192,128]{2,1,0:T(8,128)(2,1)S(1)}, bf16[8,192,128]{2,1,0:T(8,128)(2,1)S(1)}, u32[]{:S(2)}, u32[]{:S(2)}) collective-permute-start(bf16[8,192,128]{2,1,0:T(8,128)(2,1)S(1)} %get-tuple-element.11), channel_id=1, source_target_pairs={{0,1},{1,0},{2,3},{3,2},{4,5},{5,4},{6,7},{7,6},{8,9},{9,8},{10,11... | collective-permute-start | bytes 1179656 | tf_op jit(solution)/shard_map/ppermute | solution.py:396
  42.2 4.3 %collective-permute-start.1 = (bf16[8,64,128]{2,1,0:T(8,128)(2,1)S(1)}, bf16[8,64,128]{2,1,0:T(8,128)(2,1)S(1)}, u32[]{:S(2)}, u32[]{:S(2)}) collective-permute-start(bf16[8,64,128]{2,1,0:T(8,128)(2,1)S(1)} %get-tuple-element.12), channel_id=1, source_target_pairs={{0,16},{16,32},{32,48},{48,64},{64,80},{80,96},{96,112},{112,128},... | collective-permute-start | bytes 393224 | tf_op jit(solution)/shard_map/ppermute | solution.py:393
  46.5 26.3 %collective-permute-done.1.before_ref = bf16[8,64,128]{2,1,0:T(8,128)(2,1)S(1)} collective-permute-done((bf16[8,64,128]{2,1,0:T(8,128)(2,1)S(1)}, bf16[8,64,128]{2,1,0:T(8,128)(2,1)S(1)}, u32[]{:S(2)}, u32[]{:S(2)}) %collective-permute-start.1) | collective-permute-done | bytes 131104 | tf_op jit(solution)/shard_map/ppermute | solution.py:393
  72.7 1.9 %collective-permute-start.2 = (bf16[8,64,128]{2,1,0:T(8,128)(2,1)S(1)}, bf16[8,64,128]{2,1,0:T(8,128)(2,1)S(1)}, u32[]{:S(2)}, u32[]{:S(2)}) collective-permute-start(bf16[8,64,128]{2,1,0:T(8,128)(2,1)S(1)} %collective-permute-done.1.before_ref), channel_id=1, source_target_pairs={{0,1},{1,0},{2,3},{3,2},{4,5},{5,4},{6,7},{7,6},{8,9},{9,8},{10,11... | collective-permute-start | bytes 393224 | tf_op jit(solution)/shard_map/ppermute | solution.py:397
  74.7 1.3 %collective-permute-done.2.before_swap_ref = bf16[8,64,128]{2,1,0:T(8,128)(2,1)S(1)} collective-permute-done((bf16[8,64,128]{2,1,0:T(8,128)(2,1)S(1)}, bf16[8,64,128]{2,1,0:T(8,128)(2,1)S(1)}, u32[]{:S(2)}, u32[]{:S(2)}) %collective-permute-start.2) | collective-permute-done | bytes 131104 | tf_op jit(solution)/shard_map/ppermute | solution.py:397
  76.0 5.4 %shard_map.66 = (bf16[16,64,128]{2,1,0:T(8,128)(2,1)}, f32[16,32,128]{2,1,0:T(8,128)}, bf16[4,512,128]{2,1,0:T(8,128)(2,1)}) custom-call(s32[99]{0:T(128)} %concatenate.3.meta, bf16[16,192,128]{2,1,0:T(8,128)(2,1)S(1)} %all-to-all-done.in_ref, bf16[8,192,128]{2,1,0:T(8,128)(2,1)S(1)} %collective-permute-done.swap_ref, ...), custom_call_target="tpu_custom_call" | custom-call | tf_op jit(solution)/shard_map/pallas_call | solution.py:355
  81.4 7.1 %shard_map.67 = bf16[16,208,128]{2,1,0:T(8,128)(2,1)S(1)} custom-call(s32[99]{0:T(128)} %concatenate.3.meta, s32[16,32]{1,0:T(8,128)} %bitcast.9, bf16[4,512,128]{2,1,0:T(8,128)(2,1)} %get-tuple-element.13.q_buf, bf16[32,128,128]{2,1,0:T(8,128)(2,1)S(1)} %all-to-all-done.1.all_ref, bf16[16,64,128]{2,1,0:T(8,128)(2,1)} %get-tuple-element.15.slash_ref, ...), custom_call_target="tpu_custom_call" | custom-call | tf_op jit(solution)/shard_map/pallas_call | solution.py:355
  88.5 0.0 copy-start
  88.5 18.4 %all_to_all.15.in_ref = bf16[16,208,128]{2,1,0:T(8,128)(2,1)S(1)} all-to-all(bf16[16,208,128]{2,1,0:T(8,128)(2,1)S(1)} %shard_map.67), channel_id=1, replica_groups=mesh['y'=8,'k'=4,'lo'=16] {'lo'}, dimensions={0} | all-to-all | bytes 1703936 | tf_op jit(solution)/shard_map/all_to_all | solution.py:415
  106.9 2.4 %shard_map.68 = bf16[32,4096]{1,0:T(8,128)(2,1)} custom-call(s32[99]{0:T(128)} %concatenate.3.meta, bf16[16,208,128]{2,1,0:T(8,128)(2,1)S(1)} %all_to_all.15.in_ref, bf16[32,4096]{1,0:T(8,128)(2,1)S(1)} %copy-done), custom_call_target="tpu_custom_call" | custom-call | tf_op jit(solution)/shard_map/pallas_call | solution.py:355
  (11 shorter events, 0.1 us)
Async XLA Ops:
  0.0 1.0 copy-start.1
  3.1 19.9 %all-to-all-start = ((bf16[16,192,128]{2,1,0:T(8,128)(2,1)}), bf16[16,192,128]{2,1,0:T(8,128)(2,1)S(1)}, u32[]{:S(2)}, u32[]{:S(2)}) async-start(bf16[16,192,128]{2,1,0:T(8,128)(2,1)} %shard_map.64), calls=%async_computation | async-start | bytes 1572864 | tf_op jit(solution)/shard_map/all_to_all | solution.py:383
  9.4 0.7 copy-start.3
  9.4 0.7 copy-start.4
  10.1 0.7 copy-start.2
  25.0 56.4 %all-to-all-start.1 = ((bf16[32,128,128]{2,1,0:T(8,128)(2,1)}), bf16[32,128,128]{2,1,0:T(8,128)(2,1)S(1)}, u32[]{:S(2)}, u32[]{:S(2)}) async-start(bf16[32,128,128]{2,1,0:T(8,128)(2,1)} %get-tuple-element.14), calls=%async_computation.1 | async-start | bytes 2097152 | tf_op jit(solution)/shard_map/all_to_all | solution.py:394
  40.3 35.7 %collective-permute-start = (bf16[8,192,128]{2,1,0:T(8,128)(2,1)S(1)}, bf16[8,192,128]{2,1,0:T(8,128)(2,1)S(1)}, u32[]{:S(2)}, u32[]{:S(2)}) collective-permute-start(bf16[8,192,128]{2,1,0:T(8,128)(2,1)S(1)} %get-tuple-element.11), channel_id=1, source_target_pairs={{0,1},{1,0},{2,3},{3,2},{4,5},{5,4},{6,7},{7,6},{8,9},{9,8},{10,11... | collective-permute-start | bytes 1179656 | tf_op jit(solution)/shard_map/ppermute | solution.py:396
  42.2 30.5 %collective-permute-start.1 = (bf16[8,64,128]{2,1,0:T(8,128)(2,1)S(1)}, bf16[8,64,128]{2,1,0:T(8,128)(2,1)S(1)}, u32[]{:S(2)}, u32[]{:S(2)}) collective-permute-start(bf16[8,64,128]{2,1,0:T(8,128)(2,1)S(1)} %get-tuple-element.12), channel_id=1, source_target_pairs={{0,16},{16,32},{32,48},{48,64},{64,80},{80,96},{96,112},{112,128},... | collective-permute-start | bytes 393224 | tf_op jit(solution)/shard_map/ppermute | solution.py:393
  72.7 3.2 %collective-permute-start.2 = (bf16[8,64,128]{2,1,0:T(8,128)(2,1)S(1)}, bf16[8,64,128]{2,1,0:T(8,128)(2,1)S(1)}, u32[]{:S(2)}, u32[]{:S(2)}) collective-permute-start(bf16[8,64,128]{2,1,0:T(8,128)(2,1)S(1)} %collective-permute-done.1.before_ref), channel_id=1, source_target_pairs={{0,1},{1,0},{2,3},{3,2},{4,5},{5,4},{6,7},{7,6},{8,9},{9,8},{10,11... | collective-permute-start | bytes 393224 | tf_op jit(solution)/shard_map/ppermute | solution.py:397
  88.5 18.4 %copy-start = (bf16[32,4096]{1,0:T(8,128)(2,1)S(1)}, bf16[32,4096]{1,0:T(8,128)(2,1)}, u32[]{:S(2)}) copy-start(bf16[32,4096]{1,0:T(8,128)(2,1)} %gate_ref.1) | copy-start | bytes 786436
